TPU v7x, 32 devices: a whole 2x2x4 slice. The times are simulated.
32 devices in a mesh: replica: 2 (over y), shard: 2 (over x), tensor: 8 (over z, core).
Axes of the slice: x: 2, y: 2, z: 4, core: 2. Of those that a mesh axis runs over, the one named last changes fastest.
Arguments:
- layer_input: bfloat16 [32768, 1024], P(('replica', 'shard', 'tensor')), may hold values from -6 to 6
- segment_ids: int32 [32, 1024], P(('replica', 'shard')), may hold values from 0 to 3, as said below
- qkv_weight: bfloat16 [3, 1024, 1024], P(None, 'shard', 'tensor'), may hold values from -0.1875 to 0.1875
- qkv_bias: float32 [2, 1024], P(None, 'tensor'), may hold values from -1.2 to 1.2
- out_weight: bfloat16 [1024, 1024], P('tensor', 'shard'), may hold values from -1.5 to 1.5
- out_bias: float32 [1024], replicated, may hold values from -3 to 3
- norm1_gain: float32 [1024], replicated, may hold values from 0.5 to 1.5
- norm1_bias: float32 [1024], replicated, may hold values from -3 to 3
- up_weight: bfloat16 [1024, 4096], P('shard', 'tensor'), may hold values from -0.1875 to 0.1875
- up_bias: float32 [4096], P('tensor'), may hold values from -3 to 3
- down_weight: bfloat16 [4096, 1024], P('tensor', 'shard'), may hold values from -0.09375 to 0.09375
- down_bias: float32 [1024], replicated, may hold values from -3 to 3
- norm2_gain: float32 [1024], replicated, may hold values from 0.5 to 1.5
- norm2_bias: float32 [1024], replicated, may hold values from -3 to 3
- output_grad: bfloat16 [32768, 1024], P(('replica', 'shard', 'tensor')), may hold values from -6 to 6
Outputs:
- activations: bfloat16 [32768, 1024], P(('replica', 'shard', 'tensor'))
- input_grad: float32 [32768, 1024], P(('replica', 'shard', 'tensor'))
- qkv_weight_grad: float32 [3, 1024, 1024], P(None, 'shard', 'tensor')
- qkv_bias_grad: float32 [2, 1024], P(None, 'tensor')
- out_weight_grad: float32 [1024, 1024], P('tensor', 'shard')
- out_bias_grad: float32 [1024], replicated
- norm1_gain_grad: float32 [1024], replicated
- norm1_bias_grad: float32 [1024], replicated
- up_weight_grad: float32 [1024, 4096], P('shard', 'tensor')
- up_bias_grad: float32 [4096], P('tensor')
- down_weight_grad: float32 [4096, 1024], P('tensor', 'shard')
- down_bias_grad: float32 [1024], replicated
- norm2_gain_grad: float32 [1024], replicated
- norm2_bias_grad: float32 [1024], replicated
Inputs may be any that keep to these rules, and one draw needn't show every extreme that they name: `segment_ids`: within each sequence the ids never fall and every id from 0 to 3 occurs; each document holds 128 to 512 tokens, and one in each sequence holds exactly 512.
All inputs are finite; a program needn't handle non-finite values.
Results may differ from a plain program's by a relative error of at most 0.02.
Values may be sent and summed in bfloat16 or wider, within the bound.
No kernel may reach another device: no remote copies, remote signals or barrier semaphores. Data moves between devices by JAX's collectives and lax.ppermute only.
A program may use at most 256 MiB of HBM per device.

v0:
```python
import math

import jax
import jax.numpy as jnp
from jax import lax
from jax.sharding import PartitionSpec as P

HEAD_DIM = 64
LEN = 1024


EPSILON = 1e-05
NEG_FILL = -1e30
CONTRACT_ROWS = (((0,), (0,)), ((), ()))
CONTRACT_COLS = (((1,), (1,)), ((), ()))


def layer_weights(qkv_weight, out_weight, up_weight, down_weight):
    return (
        lax.all_gather(qkv_weight, "shard", axis=1, tiled=True),
        lax.all_gather(out_weight, "shard", axis=1, tiled=True),
        lax.all_gather(up_weight, "shard", axis=0, tiled=True),
        lax.all_gather(down_weight, "shard", axis=1, tiled=True),
    )


def input_rows(layer_input):
    return lax.all_gather(layer_input, "tensor", axis=0, tiled=True)


def middle_rows(hidden_low):
    return lax.all_gather(hidden_low, "tensor", axis=0, tiled=True)


def normalize(residual, gain_vec, shift_vec):
    center = residual - jnp.mean(residual, axis=-1, keepdims=True)
    spread = lax.rsqrt(jnp.mean(center * center, axis=-1, keepdims=True) + EPSILON)
    normed = center * spread
    return (normed * gain_vec + shift_vec, normed, spread)


def norm_back(incoming, normed, spread, gain_vec):
    scaled = incoming * gain_vec
    back_grad = spread * (
        scaled
        - jnp.mean(scaled, axis=-1, keepdims=True)
        - normed * jnp.mean(scaled * normed, axis=-1, keepdims=True)
    )
    return (back_grad, jnp.sum(incoming * normed, axis=0), jnp.sum(incoming, axis=0))


def masked_scores(queries, key_rows, segments):
    scores = jnp.einsum(
        "qhd,khd->hqk", queries, key_rows, preferred_element_type=jnp.float32
    ) * HEAD_DIM ** (-0.5)
    same_doc = segments[:, None] == segments[None, :]
    return jnp.where(same_doc[None], scores, NEG_FILL)


def attend(block_item):
    queries, key_rows, value_rows, segments = block_item
    scores = masked_scores(queries, key_rows, segments)
    row_max = jnp.max(scores, axis=-1, keepdims=True)
    raw_weights = jnp.exp(scores - row_max)
    row_total = jnp.sum(raw_weights, axis=-1, keepdims=True)
    attn_probs = raw_weights / row_total
    log_total = row_max + jnp.log(row_total)
    mixed_heads = jnp.einsum(
        "hqk,khd->qhd",
        attn_probs.astype(jnp.bfloat16),
        value_rows,
        preferred_element_type=jnp.float32,
    )
    return (mixed_heads.astype(jnp.bfloat16), log_total)


def attend_back(block_item):
    queries, key_rows, value_rows, segments, log_total, mixed_grad = block_item
    scores = masked_scores(queries, key_rows, segments)
    attn_probs = jnp.exp(scores - log_total)
    prob_grad = jnp.einsum(
        "qhd,khd->hqk", mixed_grad, value_rows, preferred_element_type=jnp.float32
    )
    value_grad = jnp.einsum(
        "hqk,qhd->khd",
        attn_probs.astype(jnp.bfloat16),
        mixed_grad,
        preferred_element_type=jnp.float32,
    )
    inner_sum = jnp.sum(attn_probs * prob_grad, axis=-1, keepdims=True)
    score_low = (attn_probs * (prob_grad - inner_sum)).astype(jnp.bfloat16)
    query_grad = jnp.einsum(
        "hqk,khd->qhd", score_low, key_rows, preferred_element_type=jnp.float32
    ) * HEAD_DIM ** (-0.5)
    key_grad = jnp.einsum(
        "hqk,qhd->khd", score_low, queries, preferred_element_type=jnp.float32
    ) * HEAD_DIM ** (-0.5)
    return (query_grad, key_grad, value_grad)


def body(
    layer_input,
    segment_ids,
    qkv_weight,
    qkv_bias,
    out_weight,
    out_bias,
    norm1_gain,
    norm1_bias,
    up_weight,
    up_bias,
    down_weight,
    down_bias,
    norm2_gain,
    norm2_bias,
    output_grad,
):
    rows_input = input_rows(layer_input)
    group_rows = rows_input.shape[0]
    seq_count = group_rows // LEN
    w_qkv, w_out, w_up, w_down = layer_weights(qkv_weight, out_weight, up_weight, down_weight)
    width = w_qkv.shape[2]
    heads_here = width // HEAD_DIM
    hidden_here = w_up.shape[1]

    def split_heads(rows_array):
        return rows_array.reshape(seq_count, LEN, heads_here, HEAD_DIM)

    projected = jnp.einsum("td,jdc->jtc", rows_input, w_qkv, preferred_element_type=jnp.float32)
    queries = (projected[0] + qkv_bias[0]).astype(jnp.bfloat16)
    key_rows = projected[1].astype(jnp.bfloat16)
    value_rows = (projected[2] + qkv_bias[1]).astype(jnp.bfloat16)
    mixed, log_total = lax.map(
        attend, (split_heads(queries), split_heads(key_rows), split_heads(value_rows), segment_ids)
    )
    mixed_rows = mixed.reshape(group_rows, width)
    row_block = mixed_rows
    attn_local = lax.psum_scatter(
        jnp.dot(row_block, w_out, preferred_element_type=jnp.float32).astype(jnp.bfloat16),
        "tensor",
        scatter_dimension=0,
        tiled=True,
    ).astype(jnp.float32)
    residual_one = layer_input.astype(jnp.float32) + attn_local + out_bias
    hidden_one, normed_one, spread_one = normalize(residual_one, norm1_gain, norm1_bias)
    hidden_low = hidden_one.astype(jnp.bfloat16)
    rows_middle = middle_rows(hidden_low)
    pre_act = jnp.dot(rows_middle, w_up, preferred_element_type=jnp.float32) + up_bias
    activ = jax.nn.gelu(pre_act, approximate=False).astype(jnp.bfloat16)
    row_block = activ
    mlp_local = lax.psum_scatter(
        jnp.dot(row_block, w_down, preferred_element_type=jnp.float32).astype(jnp.bfloat16),
        "tensor",
        scatter_dimension=0,
        tiled=True,
    ).astype(jnp.float32)
    residual_two = hidden_one + mlp_local + down_bias
    final_out, normed_two, spread_two = normalize(residual_two, norm2_gain, norm2_bias)
    resid_two_grad, gain_two_grad, shift_two_grad = norm_back(
        output_grad.astype(jnp.float32), normed_two, spread_two, norm2_gain
    )
    down_bias_part = jnp.sum(resid_two_grad, axis=0)
    branch_grad = resid_two_grad.astype(jnp.bfloat16)
    rows_branch = lax.all_gather(branch_grad, "tensor", axis=0, tiled=True)
    w_qkv, w_out, w_up, w_down = layer_weights(qkv_weight, out_weight, up_weight, down_weight)
    down_grad = lax.dot_general(
        activ, rows_branch, CONTRACT_ROWS, preferred_element_type=jnp.float32
    )
    activ_grad = lax.dot_general(
        rows_branch, w_down, CONTRACT_COLS, preferred_element_type=jnp.float32
    )
    normal_cdf = 0.5 * (1.0 + lax.erf(pre_act * (1.0 / math.sqrt(2.0))))
    normal_pdf = jnp.exp(-0.5 * pre_act * pre_act) * (1.0 / math.sqrt(2.0 * math.pi))
    pre_grad = activ_grad * (normal_cdf + pre_act * normal_pdf)
    up_bias_part = jnp.sum(pre_grad, axis=0)
    pre_low = pre_grad.astype(jnp.bfloat16)
    up_grad = lax.dot_general(
        rows_middle, pre_low, CONTRACT_ROWS, preferred_element_type=jnp.float32
    )
    row_block = pre_low
    back_middle = lax.psum_scatter(
        lax.dot_general(row_block, w_up, CONTRACT_COLS, preferred_element_type=jnp.float32),
        "tensor",
        scatter_dimension=0,
        tiled=True,
    )
    resid_one_grad, gain_one_grad, shift_one_grad = norm_back(
        resid_two_grad + back_middle, normed_one, spread_one, norm1_gain
    )
    out_bias_part = jnp.sum(resid_one_grad, axis=0)
    attn_grad = resid_one_grad.astype(jnp.bfloat16)
    rows_attn = lax.all_gather(attn_grad, "tensor", axis=0, tiled=True)
    out_grad_part = lax.dot_general(
        mixed_rows, rows_attn, CONTRACT_ROWS, preferred_element_type=jnp.float32
    )
    mixed_grad = lax.dot_general(
        rows_attn, w_out, CONTRACT_COLS, preferred_element_type=jnp.float32
    ).astype(jnp.bfloat16)
    query_grad, key_grad, value_grad = lax.map(
        attend_back,
        (
            split_heads(queries),
            split_heads(key_rows),
            split_heads(value_rows),
            segment_ids,
            log_total,
            split_heads(mixed_grad),
        ),
    )
    query_grad = query_grad.reshape(group_rows, width)
    key_grad = key_grad.reshape(group_rows, width)
    value_grad = value_grad.reshape(group_rows, width)
    bias_part = jnp.stack([jnp.sum(query_grad, axis=0), jnp.sum(value_grad, axis=0)])
    proj_low = jnp.stack([query_grad, key_grad, value_grad]).astype(jnp.bfloat16)
    qkv_grad = jnp.einsum("td,jtc->jdc", rows_input, proj_low, preferred_element_type=jnp.float32)
    row_block = proj_low
    back_input = lax.psum_scatter(
        jnp.einsum("jtc,jdc->td", row_block, w_qkv, preferred_element_type=jnp.float32).astype(
            jnp.bfloat16
        ),
        "tensor",
        scatter_dimension=0,
        tiled=True,
    ).astype(jnp.float32)
    input_grad = resid_one_grad + back_input
    qkv_owned, out_owned, up_owned, down_owned = (
        lax.psum_scatter(
            qkv_grad.astype(jnp.bfloat16), "shard", scatter_dimension=1, tiled=True
        ).astype(jnp.float32),
        lax.psum_scatter(
            out_grad_part.astype(jnp.bfloat16), "shard", scatter_dimension=1, tiled=True
        ).astype(jnp.float32),
        lax.psum_scatter(
            up_grad.astype(jnp.bfloat16), "shard", scatter_dimension=0, tiled=True
        ).astype(jnp.float32),
        lax.psum_scatter(
            down_grad.astype(jnp.bfloat16), "shard", scatter_dimension=1, tiled=True
        ).astype(jnp.float32),
    )
    qkv_owned, out_owned, up_owned, down_owned = (
        lax.psum(qkv_owned.astype(jnp.bfloat16), "replica").astype(jnp.float32),
        lax.psum(out_owned.astype(jnp.bfloat16), "replica").astype(jnp.float32),
        lax.psum(up_owned.astype(jnp.bfloat16), "replica").astype(jnp.float32),
        lax.psum(down_owned.astype(jnp.bfloat16), "replica").astype(jnp.float32),
    )
    tensor_index = lax.axis_index("tensor")
    tensor_count = lax.axis_size("tensor")
    bias_full = lax.dynamic_update_slice(
        jnp.zeros((2, width * tensor_count), jnp.float32),
        bias_part,
        (jnp.int32(0), tensor_index * width),
    )
    up_full = lax.dynamic_update_slice_in_dim(
        jnp.zeros((hidden_here * tensor_count,), jnp.float32),
        up_bias_part,
        tensor_index * hidden_here,
        0,
    )
    summed = lax.psum(
        (
            bias_full,
            up_full,
            out_bias_part,
            gain_one_grad,
            shift_one_grad,
            down_bias_part,
            gain_two_grad,
            shift_two_grad,
        ),
        ("replica", "shard", "tensor"),
    )
    qkv_bias_grad = lax.dynamic_slice_in_dim(summed[0], tensor_index * width, width, 1)
    up_bias_grad = lax.dynamic_slice_in_dim(summed[1], tensor_index * hidden_here, hidden_here, 0)
    return (
        final_out.astype(jnp.bfloat16),
        input_grad,
        qkv_owned,
        qkv_bias_grad,
        out_owned,
        summed[2],
        summed[3],
        summed[4],
        up_owned,
        up_bias_grad,
        down_owned,
        summed[5],
        summed[6],
        summed[7],
    )


def solution(mesh):
    placed = (
        P(("replica", "shard", "tensor"), None),
        P(("replica", "shard"), None),
        P(None, "shard", "tensor"),
        P(None, "tensor"),
        P("tensor", "shard"),
        P(),
        P(),
        P(),
        P("shard", "tensor"),
        P("tensor"),
        P("tensor", "shard"),
        P(),
        P(),
        P(),
        P(("replica", "shard", "tensor"), None),
    )
    return jax.shard_map(
        body,
        mesh=mesh,
        in_specs=placed,
        out_specs=(
            P(("replica", "shard", "tensor"), None),
            P(("replica", "shard", "tensor"), None),
            P(None, "shard", "tensor"),
            P(None, "tensor"),
            P("tensor", "shard"),
            P(),
            P(),
            P(),
            P("shard", "tensor"),
            P("tensor"),
            P("tensor", "shard"),
            P(),
            P(),
            P(),
        ),
        check_vma=False,
    )
```

profile of v0, /device:TPU:0, one launch (start us, length us, event | category | flops | bytes accessed | tf_op | source)
XLA Modules:
  0.0 2068.1 jit_solution(11723061719145368283)
XLA Ops:
  10.9 7.4 all_gather.30
  18.3 10.9 all_gather.28
  29.3 135.0 %all-gather.7.cloned.1.call-done = bf16[8192,1024]{1,0:T(8,128)(2,1)} async-done(((bf16[1024,1024]{1,0:T(8,128)(2,1)}), bf16[8192,1024]{1,0:T(8,128)(2,1)}) %all-gather.7.cloned.1.call-update) | async-done | bytes 16777232 | tf_op jit(solution)/shard_map/all_gather | solution.py:28
  164.3 13.2 fusion.73
  179.9 4.4 fusion.104
  184.3 3.6 copy.81
  187.9 3.6 copy.80
  194.1 7.1 fusion.83
  201.2 90.2 %while.26 = (s32[]{:T(128)}, bf16[8,1024,2,64]{1,3,2,0:T(8,128)(2,1)}, f32[8,2,1024,1]{2,1,3,0:T(2,128)}, bf16[8,1024,2,64]{1,3,2,0:T(8,128)(2,1)}, s32[8,1024]{...) while((s32[]{:T(128)}, ...), condition=%wide.region_3.4_spmd, body=%wide.region_0.3_spmd.sunk | while | flops 563214336 | bytes 30488676 | solution.py:133
  207.4 4.4 fusion.151
  218.7 4.4 fusion.151
  230.0 4.4 fusion.151
  241.3 4.4 fusion.151
  252.6 4.4 fusion.151
  263.8 4.4 fusion.151
  275.1 4.4 fusion.151
  286.4 4.4 fusion.151
  291.4 3.5 copy.53
  296.4 8.3 convolution_convert_fusion
  305.3 165.9 %reduce-scatter.9.cloned.1.call-done = bf16[1024,1024]{1,0:T(8,128)(2,1)} async-done(((bf16[8192,1024]{1,0:T(8,128)(2,1)}), bf16[1024,1024]{1,0:T(8,128)(2,1)}) %reduce-scatter.9.cloned.1.call-update) | async-done | bytes 2097168 | tf_op jit(solution)/shard_map/reduce_scatter | solution.py:138
  478.0 148.9 %all-gather.9.cloned.1.call-done = bf16[8192,1024]{1,0:T(8,128)(2,1)} async-done(((bf16[1024,1024]{1,0:T(8,128)(2,1)}), bf16[8192,1024]{1,0:T(8,128)(2,1)}) %all-gather.9.cloned.1.call-update) | async-done | bytes 16777232 | tf_op jit(solution)/shard_map/all_gather | solution.py:32
  626.8 47.4 %fusion.56 = (bf16[8192,512]{1,0:T(8,128)(2,1)}, f32[8192,512]{1,0:T(8,128)}) fusion(f32[512]{0:T(512)S(1)} %copy-done.31, bf16[8192,1024]{1,0:T(8,128)(2,1)} %all-gather.9.cloned.1.call-done, bf16[1024,512]{1,0:T(8,128)(2,1)} %all-gather.11.cloned.1.call-done), kind=kOutput, calls=%fused_computation.68 | convolution fusion | flops 8866758656 | bytes 42993664 | tf_op jit(solution)/shard_map/dot_general | solution.py:148
  674.2 14.8 convolution_convert_fusion.1
  689.0 166.3 %reduce-scatter.11.cloned.1.call-done = bf16[1024,1024]{1,0:T(8,128)(2,1)} async-done(((bf16[8192,1024]{1,0:T(8,128)(2,1)}), bf16[1024,1024]{1,0:T(8,128)(2,1)}) %reduce-scatter.11.cloned.1.call-update) | async-done | bytes 2097168 | tf_op jit(solution)/shard_map/reduce_scatter | solution.py:151
  855.3 4.2 fusion.103
  864.0 3.6 fusion.100
  871.4 149.7 %all-gather.15.cloned.1.call-done = bf16[8192,1024]{1,0:T(8,128)(2,1)} async-done(((bf16[1024,1024]{1,0:T(8,128)(2,1)}), bf16[8192,1024]{1,0:T(8,128)(2,1)}) %all-gather.15.cloned.1.call-update) | async-done | bytes 16777232 | tf_op jit(solution)/shard_map/all_gather | solution.py:164
  1021.1 22.2 %fusion.107 = (f32[512]{0:T(512)}, bf16[8192,512]{1,0:T(8,128)(2,1)}) fusion(f32[8192,512]{1,0:T(8,128)} %get-tuple-element.248, f32[512]{0:T(512)S(1)} %copy-done.31, bf16[8192,1024]{1,0:T(8,128)(2,1)} %all-gather.15.cloned.1.call-done, bf16[512,1024]{1,0:T(8,128)(2,1)S(1)} %copy-done.30), kind=kOutput, calls=%fused_computation.157 | convolution fusion | flops 8640266240 | bytes 42995712 | tf_op jit(solution)/shard_map/dot_general | solution.py:169
  1043.3 18.7 fusion.87
  1062.1 323.6 %reduce-scatter.13.cloned.1.call-done = f32[1024,1024]{1,0:T(8,128)} async-done(((f32[8192,1024]{1,0:T(8,128)}), f32[1024,1024]{1,0:T(8,128)}) %reduce-scatter.13.cloned.1.call-update) | async-done | bytes 4194320 | tf_op jit(solution)/shard_map/reduce_scatter | solution.py:181
  1385.7 6.6 multiply_reduce_fusion.1
  1398.6 15.9 fusion.91
  1414.7 16.2 convolution_convert_fusion.3
  1430.9 117.4 %all-gather.17.cloned.1.call-done = bf16[8192,1024]{1,0:T(8,128)(2,1)} async-done(((bf16[1024,1024]{1,0:T(8,128)(2,1)}), bf16[8192,1024]{1,0:T(8,128)(2,1)}) %all-gather.17.cloned.1.call-update) | async-done | bytes 16777232 | tf_op jit(solution)/shard_map/all_gather | solution.py:192
  1548.3 8.3 convolution_convert_fusion.2
  1556.7 3.3 reshape.197
  1560.0 9.1 copy.56
  1569.1 160.9 %while.27 = (s32[]{:T(128)}, f32[8,1024,2,64]{1,3,2,0:T(8,128)}, bf16[8,1024,2,64]{1,3,2,0:T(8,128)(2,1)}, f32[8,1024,2,64]{1,3,2,0:T(8,128)}, bf16[8,1024,2,64]...) while((s32[]{:T(128)}, f32[8,1024,2,64]{1,3,2,0:T(8,128)}, ...), condition=%wide.region_17.18_spmd, body=%wide.region_15.17_spmd.sunk | while | flops 1374943232 | bytes 70591616 | solution.py:199
  1577.1 3.9 multiply_reduce_fusion.7
  1593.8 3.3 fusion.163
  1597.2 3.9 multiply_reduce_fusion.7
  1617.3 3.9 multiply_reduce_fusion.7
  1634.0 3.3 fusion.163
  1637.4 3.9 multiply_reduce_fusion.7
  1657.5 3.9 multiply_reduce_fusion.7
  1674.2 3.3 fusion.163
  1677.5 3.9 multiply_reduce_fusion.7
  1697.6 3.9 multiply_reduce_fusion.7
  1714.3 3.3 fusion.163
  1717.7 3.9 multiply_reduce_fusion.7
  1730.0 4.2 fusion.106
  1736.5 10.8 copy.74
  1747.3 8.2 reshape.198
  1755.5 7.3 copy.76
  1762.8 7.9 reshape.200
  1770.7 7.3 copy.75
  1778.1 7.9 reshape.199
  1789.1 8.8 convolution_convert_fusion.4
  1802.6 13.0 fusion.97
  1815.7 15.7 reduce-scatter.17.cloned.1.call-done
  1831.4 14.5 bitcast_convert_fusion
  1847.0 41.2 %all-reduce = (f32[2,1024]{1,0:T(2,128)S(1)}, f32[1024]{0:T(1024)}, f32[1024]{0:T(1024)}, f32[1024]{0:T(1024)}, f32[4096]{0:T(1024)S(1)}, /*index=5*/f32[1024]{0:T(1024)}, f32[1024]{0:T(1024)}, f32[1024]{0:T(1024)}) all-reduce(f32[2,1024]{1,0:T(2,128)S(1)} %maximum_dynamic-update-sl, ...), channel_id=1, replica_groups=mesh['replica'=2,'shard'=2,'tensor'=8] {'replica','shard','tensor'}, use_global_device_ids=true, to_apply=%region_23.24 | all-reduce | flops 12288 | bytes 98304 | tf_op jit(solution)/shard_map/psum | solution.py:259
  1897.5 156.9 %reduce-scatter.15.cloned.1.call-done = bf16[1024,1024]{1,0:T(8,128)(2,1)} async-done(((bf16[8192,1024]{1,0:T(8,128)(2,1)}), bf16[1024,1024]{1,0:T(8,128)(2,1)}) %reduce-scatter.15.cloned.1.call-update) | async-done | bytes 2097168 | tf_op jit(solution)/shard_map/reduce_scatter | solution.py:217
  2054.4 5.9 convert_add_fusion
  (245 shorter events, 222.5 us)
Async XLA Ops:
  8.0 156.2 %all-gather.7.cloned.1.call-start = ((), (), s32[]{:S(2)}) async-start(), calls=%async_computation.8 | async-start | bytes 18874368 | tf_op jit(solution)/shard_map/all_gather | solution.py:28
  8.7 462.5 %reduce-scatter.9.cloned.1.call-start = ((), (), s32[]{:S(2)}) async-start(), calls=%async_computation.9 | async-start | bytes 18874368 | tf_op jit(solution)/shard_map/reduce_scatter | solution.py:138
  18.3 278.0 %copy-start.12 = (bf16[128,1024]{1,0:T(8,128)(2,1)}, bf16[128,1024]{1,0:T(8,128)(2,1)S(1)}, u32[]{:S(2)}) copy-start(bf16[128,1024]{1,0:T(8,128)(2,1)S(1)} %all_gather.30) | copy-start | bytes 786436
  29.2 148.2 %copy-start.14 = (bf16[3,1024,128]{1,2,0:T(8,128)(2,1)}, bf16[3,1024,128]{1,2,0:T(8,128)(2,1)S(1)}, u32[]{:S(2)}) copy-start(bf16[3,1024,128]{1,2,0:T(8,128)(2,1)S(1)} %all_gather.28) | copy-start | bytes 2359300
  291.4 3.5 copy-start.7
  296.3 8.3 copy-start.5
  304.6 166.6 %copy-start = (bf16[1024,1024]{1,0:T(8,128)(2,1)S(1)}, bf16[1024,1024]{1,0:T(8,128)(2,1)}, u32[]{:S(2)}) copy-start(bf16[1024,1024]{1,0:T(8,128)(2,1)} %param.19) | copy-start | bytes 6291460
  304.7 166.6 %copy-start.16 = (f32[1024]{0:T(1024)S(1)}, f32[1024]{0:T(1024)}, u32[]{:S(2)}) copy-start(f32[1024]{0:T(1024)} %param.24) | copy-start | bytes 12292
  304.7 173.3 %all-gather.11.cloned.1.call-start = ((), (), s32[]{:S(2)}) async-start(), calls=%async_computation.11 | async-start | bytes 1572864 | tf_op jit(solution)/shard_map/all_gather | solution.py:22
  305.3 169.5 %copy-start.17 = (f32[1024]{0:T(1024)S(1)}, f32[1024]{0:T(1024)}, u32[]{:S(2)}) copy-start(f32[1024]{0:T(1024)} %param.25) | copy-start | bytes 12292
  305.3 169.5 %copy-start.21 = (f32[1024]{0:T(1024)S(1)}, f32[1024]{0:T(1024)}, u32[]{:S(2)}) copy-start(f32[1024]{0:T(1024)} %param.26) | copy-start | bytes 12292
  305.3 321.6 %all-gather.9.cloned.1.call-start = ((), (), s32[]{:S(2)}) async-start(), calls=%async_computation.10 | async-start | bytes 18874368 | tf_op jit(solution)/shard_map/all_gather | solution.py:32
  471.2 2.5 copy-start.1
  474.8 152.0 %copy-start.31 = (f32[512]{0:T(512)S(1)}, f32[512]{0:T(512)}, u32[]{:S(2)}) copy-start(f32[512]{0:T(512)} %param.28) | copy-start | bytes 6148
  477.3 196.9 %all-gather.13.cloned.1.call-start = ((), (), s32[]{:S(2)}) async-start(), calls=%async_computation.12 | async-start | bytes 1572864 | tf_op jit(solution)/shard_map/all_gather | solution.py:23
  477.9 377.5 %reduce-scatter.11.cloned.1.call-start = ((), (), s32[]{:S(2)}) async-start(), calls=%async_computation.13 | async-start | bytes 18874368 | tf_op jit(solution)/shard_map/reduce_scatter | solution.py:151
  689.0 166.4 %copy-start.27 = (f32[1024]{0:T(1024)S(1)}, f32[1024]{0:T(1024)}, u32[]{:S(2)}) copy-start(f32[1024]{0:T(1024)} %param.30) | copy-start | bytes 12292
  689.0 332.1 %all-gather.15.cloned.1.call-start = ((), (), s32[]{:S(2)}) async-start(), calls=%async_computation.14 | async-start | bytes 18874368 | tf_op jit(solution)/shard_map/all_gather | solution.py:164
  859.6 1.6 copy-start.8
  859.6 1.6 copy-start.20
  860.2 3.9 copy-start.26
  867.6 2.0 copy-start.4
  869.6 151.5 %copy-start.30 = (bf16[512,1024]{1,0:T(8,128)(2,1)S(1)}, bf16[512,1024]{1,0:T(8,128)(2,1)}, u32[]{:S(2)}) copy-start(bf16[512,1024]{1,0:T(8,128)(2,1)} %all-gather.13.cloned.1.call-done) | copy-start | bytes 3145732
  871.3 514.4 %reduce-scatter.13.cloned.1.call-start = ((), (), s32[]{:S(2)}) async-start(), calls=%async_computation.15 | async-start | bytes 37748736 | tf_op jit(solution)/shard_map/reduce_scatter | solution.py:181
  1021.1 22.3 %copy-start.29 = (bf16[1024,512]{1,0:T(8,128)(2,1)S(1)}, bf16[1024,512]{1,0:T(8,128)(2,1)}, u32[]{:S(2)}) copy-start(bf16[1024,512]{1,0:T(8,128)(2,1)} %all-gather.11.cloned.1.call-done) | copy-start | bytes 3145732
  1062.1 486.2 %all-gather.17.cloned.1.call-start = ((), (), s32[]{:S(2)}) async-start(), calls=%async_computation.16 | async-start | bytes 18874368 | tf_op jit(solution)/shard_map/all_gather | solution.py:192
  1385.7 6.6 copy-start.2
  1394.9 2.0 copy-start.3
  1398.5 417.1 %reduce-scatter.21.cloned.1.call-start = ((), (), s32[]{:S(2)}) async-start(), calls=%async_computation.20 | async-start | bytes 1572864 | tf_op jit(solution)/shard_map/reduce_scatter | solution.py:233
  1414.6 133.7 %copy-start.13 = (bf16[128,1024]{1,0:T(8,128)(2,1)S(1)}, bf16[128,1024]{1,0:T(8,128)(2,1)}, u32[]{:S(2)}) copy-start(bf16[128,1024]{1,0:T(8,128)(2,1)} %copy-done.12) | copy-start | bytes 786436
  1414.6 401.0 %reduce-scatter.23.cloned.1.call-start = ((), (), s32[]{:S(2)}) async-start(), calls=%async_computation.21 | async-start | bytes 1572864 | tf_op jit(solution)/shard_map/reduce_scatter | solution.py:236
  1430.8 384.8 %reduce-scatter.19.cloned.1.call-start = ((), (), s32[]{:S(2)}) async-start(), calls=%async_computation.19 | async-start | bytes 393216 | tf_op jit(solution)/shard_map/reduce_scatter | solution.py:230
  1730.0 4.6 copy-start.10
  1762.8 7.9 copy-start.11
  1778.1 11.0 copy-start.6
  1797.9 3.2 copy-start.9
  1797.9 33.5 %reduce-scatter.17.cloned.1.call-start = ((), (), s32[]{:S(2)}) async-start(), calls=%async_computation.18 | async-start | bytes 1179648 | tf_op jit(solution)/shard_map/reduce_scatter | solution.py:227
  1802.6 28.9 %copy-start.15 = (bf16[3,1024,128]{1,2,0:T(8,128)(2,1)S(1)}, bf16[3,1024,128]{1,2,0:T(8,128)(2,1)}, u32[]{:S(2)}) copy-start(bf16[3,1024,128]{1,2,0:T(8,128)(2,1)} %copy-done.14) | copy-start | bytes 2359300
  1815.6 73.9 %all-reduce.4.cloned.1.call-start = ((), (), s32[]{:S(2)}) async-start(), calls=%async_computation.22 | async-start | bytes 3145728 | tf_op jit(solution)/shard_map/psum | solution.py:241
  1831.4 223.0 %reduce-scatter.15.cloned.1.call-start = ((), (), s32[]{:S(2)}) async-start(), calls=%async_computation.17 | async-start | bytes 18874368 | tf_op jit(solution)/shard_map/reduce_scatter | solution.py:217
  1845.9 0.7 copy-start.28
  1845.9 1.0 copy-start.18
  1845.9 1.0 copy-start.19
  1845.9 1.1 copy-start.22
  1846.0 1.1 copy-start.23
  1846.0 1.1 copy-start.24
  1846.0 1.1 copy-start.25
Sparse Core Ops, SparseCore 0:
  10.4 153.7 all-gather.6
  304.8 166.3 reduce-scatter.8
  871.4 149.5 all-gather.14
  1398.7 149.6 all-gather.16
  1831.5 52.2 all-reduce.3
  1886.0 168.3 reduce-scatter.14
Sparse Core Ops, SparseCore 1:
  306.7 19.3 all-gather.10
  477.4 149.4 all-gather.8
  628.3 19.3 all-gather.12
  689.1 166.2 reduce-scatter.10
  1062.2 323.5 reduce-scatter.12
  1414.7 18.5 reduce-scatter.20
  1435.9 20.3 reduce-scatter.22
  1798.0 9.8 reduce-scatter.18
  1815.6 15.7 reduce-scatter.16
where the time goes:
time: 2080 us; the launch traced here: 2070 us
  waiting for transfers between devices  1380 us (66%)
  matrix products  381 us (18%)
  local copies, waits for them, and re-layouts  121 us (6%)
  other arithmetic  108 us (5%)
  blocking collectives  59.6 us (3%)
    reduce_scatter x1, waiting for transfers between devices, body(): lax.psum_scatter(lax.dot_general(row_block, w_up, CONTRACT_COLS, preferre...  324 us
    reduce_scatter x1, waiting for transfers between devices, body(): lax.psum_scatter(jnp.dot(row_block, w_down, preferred_element_type=jnp.fl...  166 us
    reduce_scatter x1, waiting for transfers between devices, body(): lax.psum_scatter(jnp.dot(row_block, w_out, preferred_element_type=jnp.flo...  166 us
    reduce_scatter x1, waiting for transfers between devices, body(): lax.psum_scatter(jnp.einsum('jtc,jdc->td', row_block, w_qkv, preferred_el...  157 us
    all_gather x1, waiting for transfers between devices, body(): rows_branch = lax.all_gather(branch_grad, 'tensor', axis=0, tiled=True)  150 us
    all_gather x1, waiting for transfers between devices, middle_rows(): return lax.all_gather(hidden_low, 'tensor', axis=0, tiled=True)  149 us
    all_gather x1, waiting for transfers between devices, input_rows(): return lax.all_gather(layer_input, 'tensor', axis=0, tiled=True)  135 us
    all_gather x1, waiting for transfers between devices, body(): rows_attn = lax.all_gather(attn_grad, 'tensor', axis=0, tiled=True)  117 us
  transfers between devices with their start and end apart: 15, of which 9 were waited for; matrix products, arithmetic and copies ran while one was open for 18% of the time, Pallas kernels for 0%

commit v1 on v0

v1 whole, which is shorter than its diff:
```python
import math

import jax
import jax.numpy as jnp
from jax import lax
from jax.sharding import PartitionSpec as P

HEAD_DIM = 64
LEN = 1024

EPSILON = 1e-05
NEG_FILL = -1e30
CONTRACT_ROWS = (((0,), (0,)), ((), ()))
CONTRACT_COLS = (((1,), (1,)), ((), ()))
OWNERS = ("shard", "tensor")
EVERYONE = ("replica", "shard", "tensor")


def gather_blocks(weight):
    blocks = lax.all_gather(weight, OWNERS, axis=0, tiled=False)
    return blocks.reshape((lax.axis_size("shard"), lax.axis_size("tensor")) + weight.shape)


def gather_qkv(weight):
    blocks = gather_blocks(weight)
    return blocks.transpose(2, 0, 3, 1, 4).reshape(3, -1, blocks.shape[1] * blocks.shape[4])


def gather_row_col(weight):
    blocks = gather_blocks(weight)
    return blocks.transpose(0, 2, 1, 3).reshape(-1, blocks.shape[1] * blocks.shape[3])


def gather_col_row(weight):
    blocks = gather_blocks(weight)
    return blocks.transpose(1, 2, 0, 3).reshape(-1, blocks.shape[0] * blocks.shape[3])


def scatter_blocks(blocks):
    flat = blocks.reshape((-1,) + blocks.shape[2:])
    owned = lax.psum_scatter(flat, OWNERS, scatter_dimension=0, tiled=False)
    return lax.psum(owned, "replica").astype(jnp.float32)


def scatter_qkv(grad):
    shards, tensors = lax.axis_size("shard"), lax.axis_size("tensor")
    three, rows, cols = grad.shape
    blocks = grad.reshape(three, shards, rows // shards, tensors, cols // tensors)
    return scatter_blocks(blocks.transpose(1, 3, 0, 2, 4))


def scatter_row_col(grad):
    shards, tensors = lax.axis_size("shard"), lax.axis_size("tensor")
    rows, cols = grad.shape
    blocks = grad.reshape(shards, rows // shards, tensors, cols // tensors)
    return scatter_blocks(blocks.transpose(0, 2, 1, 3))


def scatter_col_row(grad):
    shards, tensors = lax.axis_size("shard"), lax.axis_size("tensor")
    rows, cols = grad.shape
    blocks = grad.reshape(tensors, rows // tensors, shards, cols // shards)
    return scatter_blocks(blocks.transpose(2, 0, 1, 3))


def normalize(residual, gain_vec, shift_vec):
    center = residual - jnp.mean(residual, axis=-1, keepdims=True)
    spread = lax.rsqrt(jnp.mean(center * center, axis=-1, keepdims=True) + EPSILON)
    normed = center * spread
    return (normed * gain_vec + shift_vec, normed, spread)


def norm_back(incoming, normed, spread, gain_vec):
    scaled = incoming * gain_vec
    back_grad = spread * (
        scaled
        - jnp.mean(scaled, axis=-1, keepdims=True)
        - normed * jnp.mean(scaled * normed, axis=-1, keepdims=True)
    )
    return (back_grad, jnp.sum(incoming * normed, axis=0), jnp.sum(incoming, axis=0))


def masked_scores(queries, key_rows, same_doc):
    scores = jnp.einsum(
        "qhd,khd->hqk", queries, key_rows, preferred_element_type=jnp.float32
    ) * HEAD_DIM ** (-0.5)
    return jnp.where(same_doc[None], scores, NEG_FILL)


def attend(queries, key_rows, value_rows, same_doc):
    scores = masked_scores(queries, key_rows, same_doc)
    row_max = jnp.max(scores, axis=-1, keepdims=True)
    raw_weights = jnp.exp(scores - row_max)
    row_total = jnp.sum(raw_weights, axis=-1, keepdims=True)
    attn_probs = raw_weights / row_total
    log_total = row_max + jnp.log(row_total)
    mixed_heads = jnp.einsum(
        "hqk,khd->qhd",
        attn_probs.astype(jnp.bfloat16),
        value_rows,
        preferred_element_type=jnp.float32,
    )
    return (mixed_heads.astype(jnp.bfloat16), log_total)


def attend_back(queries, key_rows, value_rows, same_doc, log_total, mixed_grad):
    scores = masked_scores(queries, key_rows, same_doc)
    attn_probs = jnp.exp(scores - log_total)
    prob_grad = jnp.einsum(
        "qhd,khd->hqk", mixed_grad, value_rows, preferred_element_type=jnp.float32
    )
    value_grad = jnp.einsum(
        "hqk,qhd->khd",
        attn_probs.astype(jnp.bfloat16),
        mixed_grad,
        preferred_element_type=jnp.float32,
    )
    inner_sum = jnp.sum(attn_probs * prob_grad, axis=-1, keepdims=True)
    score_low = (attn_probs * (prob_grad - inner_sum)).astype(jnp.bfloat16)
    query_grad = jnp.einsum(
        "hqk,khd->qhd", score_low, key_rows, preferred_element_type=jnp.float32
    ) * HEAD_DIM ** (-0.5)
    key_grad = jnp.einsum(
        "hqk,qhd->khd", score_low, queries, preferred_element_type=jnp.float32
    ) * HEAD_DIM ** (-0.5)
    return (query_grad, key_grad, value_grad)


def body(
    layer_input,
    segment_ids,
    qkv_weight,
    qkv_bias,
    out_weight,
    out_bias,
    norm1_gain,
    norm1_bias,
    up_weight,
    up_bias,
    down_weight,
    down_bias,
    norm2_gain,
    norm2_bias,
    output_grad,
):
    rows, width = layer_input.shape
    tensor_index = lax.axis_index("tensor")
    tensor_count = lax.axis_size("tensor")
    sharers = max(1, LEN // rows)
    seqs_here = max(1, rows // LEN)
    query_rows = min(rows, LEN)
    sharing = [list(range(i, i + sharers)) for i in range(0, tensor_count, sharers)]

    w_qkv = gather_qkv(qkv_weight)
    bias_qkv = lax.all_gather(qkv_bias, "tensor", axis=1, tiled=True)
    bias_up = lax.all_gather(up_bias, "tensor", axis=0, tiled=True)
    w_out = gather_col_row(out_weight)
    w_up = gather_row_col(up_weight)
    w_down = gather_col_row(down_weight)

    first_seq = tensor_index * rows // LEN
    key_segments = lax.dynamic_slice_in_dim(segment_ids, first_seq, seqs_here, 0)
    query_start = tensor_index * rows % LEN
    query_segments = lax.dynamic_slice_in_dim(key_segments, query_start, query_rows, 1)
    same_doc = query_segments[:, :, None] == key_segments[:, None, :]

    heads = width // HEAD_DIM
    group = 2

    def by_head(rows_array, length):
        split = rows_array.reshape(seqs_here, length, heads // group, group, HEAD_DIM)
        return split.transpose(0, 2, 1, 3, 4)

    def from_heads(blocks):
        return blocks.transpose(0, 2, 1, 3, 4).reshape(-1, width)

    def whole_rows(rows_array):
        if sharers == 1:
            return rows_array
        return lax.all_gather(rows_array, "tensor", axis_index_groups=sharing, axis=0, tiled=True)

    def own_rows(rows_array):
        if sharers == 1:
            return rows_array
        return lax.psum_scatter(
            rows_array, "tensor", axis_index_groups=sharing, scatter_dimension=0, tiled=True
        )

    projected = jnp.einsum("td,jdc->jtc", layer_input, w_qkv, preferred_element_type=jnp.float32)
    queries = (projected[0] + bias_qkv[0]).astype(jnp.bfloat16)
    key_rows = whole_rows(projected[1].astype(jnp.bfloat16))
    value_rows = whole_rows((projected[2] + bias_qkv[1]).astype(jnp.bfloat16))
    queries = by_head(queries, query_rows)
    key_rows = by_head(key_rows, LEN)
    value_rows = by_head(value_rows, LEN)
    mixed, log_total = [], []
    for s in range(seqs_here):
        one_mixed, one_log = lax.map(
            lambda item: attend(*item, same_doc[s]), (queries[s], key_rows[s], value_rows[s])
        )
        mixed.append(one_mixed)
        log_total.append(one_log)
    mixed_rows = from_heads(jnp.stack(mixed))
    residual_one = (
        layer_input.astype(jnp.float32)
        + jnp.dot(mixed_rows, w_out, preferred_element_type=jnp.float32)
        + out_bias
    )
    hidden_one, normed_one, spread_one = normalize(residual_one, norm1_gain, norm1_bias)
    hidden_low = hidden_one.astype(jnp.bfloat16)
    pre_act = jnp.dot(hidden_low, w_up, preferred_element_type=jnp.float32) + bias_up
    activ = jax.nn.gelu(pre_act, approximate=False).astype(jnp.bfloat16)
    residual_two = (
        hidden_one + jnp.dot(activ, w_down, preferred_element_type=jnp.float32) + down_bias
    )
    final_out, normed_two, spread_two = normalize(residual_two, norm2_gain, norm2_bias)
    resid_two_grad, gain_two_grad, shift_two_grad = norm_back(
        output_grad.astype(jnp.float32), normed_two, spread_two, norm2_gain
    )
    down_bias_part = jnp.sum(resid_two_grad, axis=0)
    branch_grad = resid_two_grad.astype(jnp.bfloat16)
    down_grad = lax.dot_general(
        activ, branch_grad, CONTRACT_ROWS, preferred_element_type=jnp.float32
    ).astype(jnp.bfloat16)
    down_owned = scatter_col_row(down_grad)
    activ_grad = lax.dot_general(
        branch_grad, w_down, CONTRACT_COLS, preferred_element_type=jnp.float32
    )
    normal_cdf = 0.5 * (1.0 + lax.erf(pre_act * (1.0 / math.sqrt(2.0))))
    normal_pdf = jnp.exp(-0.5 * pre_act * pre_act) * (1.0 / math.sqrt(2.0 * math.pi))
    pre_grad = activ_grad * (normal_cdf + pre_act * normal_pdf)
    up_bias_part = jnp.sum(pre_grad, axis=0)
    pre_low = pre_grad.astype(jnp.bfloat16)
    up_grad = lax.dot_general(
        hidden_low, pre_low, CONTRACT_ROWS, preferred_element_type=jnp.float32
    ).astype(jnp.bfloat16)
    up_owned = scatter_row_col(up_grad)
    back_middle = lax.dot_general(pre_low, w_up, CONTRACT_COLS, preferred_element_type=jnp.float32)
    resid_one_grad, gain_one_grad, shift_one_grad = norm_back(
        resid_two_grad + back_middle, normed_one, spread_one, norm1_gain
    )
    out_bias_part = jnp.sum(resid_one_grad, axis=0)
    attn_grad = resid_one_grad.astype(jnp.bfloat16)
    out_grad = lax.dot_general(
        mixed_rows, attn_grad, CONTRACT_ROWS, preferred_element_type=jnp.float32
    ).astype(jnp.bfloat16)
    out_owned = scatter_col_row(out_grad)
    mixed_grad = lax.dot_general(
        attn_grad, w_out, CONTRACT_COLS, preferred_element_type=jnp.float32
    ).astype(jnp.bfloat16)
    mixed_grad = by_head(mixed_grad, query_rows)
    query_grad, key_grad, value_grad = [], [], []
    for s in range(seqs_here):
        grads = lax.map(
            lambda item: attend_back(item[0], item[1], item[2], same_doc[s], item[3], item[4]),
            (queries[s], key_rows[s], value_rows[s], log_total[s], mixed_grad[s]),
        )
        query_grad.append(grads[0])
        key_grad.append(grads[1])
        value_grad.append(grads[2])
    query_grad = from_heads(jnp.stack(query_grad))
    key_grad = own_rows(from_heads(jnp.stack(key_grad)))
    value_grad = own_rows(from_heads(jnp.stack(value_grad)))
    proj_low = [grad.astype(jnp.bfloat16) for grad in (query_grad, key_grad, value_grad)]
    qkv_grad = jnp.stack(
        [
            lax.dot_general(
                layer_input, grad, CONTRACT_ROWS, preferred_element_type=jnp.float32
            ).astype(jnp.bfloat16)
            for grad in proj_low
        ]
    )
    qkv_owned = scatter_qkv(qkv_grad)
    input_grad = resid_one_grad
    for j in range(3):
        input_grad = input_grad + lax.dot_general(
            proj_low[j], w_qkv[j], CONTRACT_COLS, preferred_element_type=jnp.float32
        )
    parts = (
        jnp.sum(query_grad, axis=0),
        jnp.sum(value_grad, axis=0),
        up_bias_part,
        out_bias_part,
        gain_one_grad,
        shift_one_grad,
        down_bias_part,
        gain_two_grad,
        shift_two_grad,
    )
    summed = jnp.sum(lax.all_gather(jnp.concatenate(parts), EVERYONE, axis=0, tiled=False), axis=0)
    ends = [0]
    for part in parts:
        ends.append(ends[-1] + part.shape[0])
    summed = [summed[ends[i] : ends[i + 1]] for i in range(len(parts))]
    width_here = qkv_bias.shape[1]
    hidden_here = up_bias.shape[0]
    qkv_bias_grad = lax.dynamic_slice_in_dim(
        jnp.stack(summed[:2]), tensor_index * width_here, width_here, 1
    )
    up_bias_grad = lax.dynamic_slice_in_dim(summed[2], tensor_index * hidden_here, hidden_here, 0)
    return (
        final_out.astype(jnp.bfloat16),
        input_grad,
        qkv_owned,
        qkv_bias_grad,
        out_owned,
        summed[3],
        summed[4],
        summed[5],
        up_owned,
        up_bias_grad,
        down_owned,
        summed[6],
        summed[7],
        summed[8],
    )


def solution(mesh):
    placed = (
        P(("replica", "shard", "tensor"), None),
        P(("replica", "shard"), None),
        P(None, "shard", "tensor"),
        P(None, "tensor"),
        P("tensor", "shard"),
        P(),
        P(),
        P(),
        P("shard", "tensor"),
        P("tensor"),
        P("tensor", "shard"),
        P(),
        P(),
        P(),
        P(("replica", "shard", "tensor"), None),
    )
    return jax.shard_map(
        body,
        mesh=mesh,
        in_specs=placed,
        out_specs=(
            P(("replica", "shard", "tensor"), None),
            P(("replica", "shard", "tensor"), None),
            P(None, "shard", "tensor"),
            P(None, "tensor"),
            P("tensor", "shard"),
            P(),
            P(),
            P(),
            P("shard", "tensor"),
            P("tensor"),
            P("tensor", "shard"),
            P(),
            P(),
            P(),
        ),
        check_vma=False,
    )
```

time: 2080 us -> 1100 us (0.53)
  waiting for transfers between devices: 1380 us -> 358 us
  local copies, waits for them, and re-layouts: 121 us -> 222 us
  blocking collectives: 59.6 us -> 26.5 us
    reduce_scatter x8 -> x4, waiting for transfers between devices: 828 us -> 197 us  [scatter_blocks(): owned = lax.psum_scatter(flat, OWNERS, scatter_dimension=0, tiled=False)]
    all_gather x6 -> x5, waiting for transfers between devices: 551 us -> 109 us  [the longest x4 69.3 us: gather_blocks(): blocks = lax.all_gather(weight, OWNERS, axis=0, tiled=False)]
    reshape x1 -> x7, local copies, waits for them, and re-layouts: 3.32 us -> 77.9 us  [the longest x4 46.9 us: gather_blocks(): blocks.reshape((lax.axis_size('shard'), lax.axis_size('tensor')) + weight...]
    psum x1, waiting for transfers between devices: 0.01 us -> 49.2 us  [scatter_blocks(): return lax.psum(owned, 'replica').astype(jnp.float32)]
    transpose x0 -> x5, local copies, waits for them, and re-layouts: none -> 45.3 us  [the longest x2 17.1 us: scatter_row_col(): return scatter_blocks(blocks.transpose(0, 2, 1, 3))]
    psum x1 -> x0, blocking collectives: 41.2 us -> none  [body(): lax.psum((bias_full, up_full, out_bias_part, gain_one_grad, shift_one_gra...]
    unnamed x72 -> x132, local copies, waits for them, and re-layouts: 25.6 us -> 66.8 us
    another operation x9 -> x3, local copies, waits for them, and re-layouts: 51.1 us -> 12.4 us  [body(): jnp.stack([lax.dot_general(layer_input, grad, CONTRACT_ROWS, preferred_el...]
  transfers between devices with their start and end apart: 15 -> 10, of which waited for: 9 -> 6; matrix products, arithmetic and copies ran while one was open for 18% -> 33% of each run, Pallas kernels for 0% -> 0%
where the time goes in v1:
time: 1100 us; the launch traced here: 1080 us
  matrix products  363 us (33%)
  waiting for transfers between devices  358 us (33%)
  local copies, waits for them, and re-layouts  222 us (20%)
  other arithmetic  98.6 us (9%)
  blocking collectives  26.5 us (2%)
  between operations  15.4 us (1%)
    reduce_scatter x4, waiting for transfers between devices, scatter_blocks(): owned = lax.psum_scatter(flat, OWNERS, scatter_dimension=0, tiled=False)  197 us
    all_gather x4, waiting for transfers between devices, gather_blocks(): blocks = lax.all_gather(weight, OWNERS, axis=0, tiled=False)  69.3 us
    unnamed x132, local copies, waits for them, and re-layouts  66.8 us
    psum x1, waiting for transfers between devices, scatter_blocks(): return lax.psum(owned, 'replica').astype(jnp.float32)  49.2 us
    dot_general x1, matrix products, body(): jnp.dot(hidden_low, w_up, preferred_element_type=jnp.float32) + bias_up  47.6 us
    reshape x4, local copies, waits for them, and re-layouts, gather_blocks(): blocks.reshape((lax.axis_size('shard'), lax.axis_size('tensor')) + weight...  46.9 us
    dot_general x16, matrix products, masked_scores(): jnp.einsum('qhd,khd->hqk', queries, key_rows, preferred_element_type=jnp....  41.3 us
    all_gather x1, waiting for transfers between devices, body(): lax.all_gather(jnp.concatenate(parts), EVERYONE, axis=0, tiled=False)  39.8 us
  transfers between devices with their start and end apart: 10, of which 6 were waited for; matrix products, arithmetic and copies ran while one was open for 33% of the time, Pallas kernels for 0%

profile of v1, /device:TPU:0, one launch (start us, length us, event | category | flops | bytes accessed | tf_op | source)
XLA Modules:
  0.0 1084.6 jit_solution(9665924579139208757)
XLA Ops:
  10.1 13.7 %all_gather.38 = f32[2,1024]{1,0:T(2,128)S(1)} all-gather(f32[2,128]{1,0:T(2,128)} %param.22), channel_id=1, replica_groups=mesh['replica'=2,'shard'=2,'tensor'=8] {'tensor'}, dimensions={1}, use_global_device_ids=true | all-gather | bytes 9216 | tf_op jit(solution)/shard_map/all_gather | solution.py:155
  24.0 3.9 copy.93
  28.0 12.8 %all-gather.5 = f32[8,1,512]{2,1,0:T(1,128)S(1)} all-gather(f32[1,1,512]{2,1,0:T(1,128)S(1)} %bitcast.312), channel_id=1, replica_groups=mesh['replica'=2,'shard'=2,'tensor'=8] {'tensor'}, dimensions={0}, use_global_device_ids=true | all-gather | bytes 18432 | tf_op jit(solution)/shard_map/all_gather | solution.py:156
  43.3 11.1 %all-gather.14.cloned.1.call-done = bf16[2048,512]{1,0:T(8,128)(2,1)} async-done(((bf16[128,512]{1,0:T(8,128)(2,1)}), bf16[2048,512]{1,0:T(8,128)(2,1)}) %all-gather.14.cloned.1.call-update) | async-done | bytes 2097168 | tf_op jit(solution)/shard_map/all_gather | solution.py:20
  54.4 4.3 copy.95
  58.8 58.2 %all-gather.12.cloned.1.call-done = bf16[48,512,128]{2,1,0:T(8,128)(2,1)} async-done(((bf16[3,512,128]{2,1,0:T(8,128)(2,1)}), bf16[48,512,128]{2,1,0:T(8,128)(2,1)}) %all-gather.12.cloned.1.call-update) | async-done | bytes 6291472 | tf_op jit(solution)/shard_map/all_gather | solution.py:20
  116.9 16.2 %copy.94 = bf16[2,8,3,512,128]{3,0,4,1,2:T(2,128)(2,1)} copy(bf16[2,8,3,512,128]{4,3,2,1,0:T(8,128)(2,1)} %bitcast.294) | data formatting | bytes 12582912 | tf_op jit(solution)/shard_map/reshape | solution.py:21
  133.1 11.0 %reshape.287 = bf16[3,1024,1024]{1,2,0:T(8,128)(2,1)} reshape(bf16[3,2,512,8,128]{2,1,4,3,0:T(2,128)(2,1)} %bitcast.265) | data formatting | bytes 12582912 | tf_op jit(solution)/shard_map/reshape | solution.py:26
  144.1 9.7 convolution_bitcast_fusion
  153.8 4.5 copy-done.13
  165.1 84.4 %while.28 = (s32[]{:T(128)}, bf16[8,1024,2,64]{1,3,2,0:T(8,128)(2,1)}, f32[8,2,1024,1]{2,1,3,0:T(2,128)}, bf16[8,1024,2,64]{1,3,2,0:T(8,128)(2,1)}, bf16[8,1024,...) while((s32[]{:T(128)}, ...), condition=%wide.region_3.4_spmd.clone, body=%wide.region_0.3_spmd.clone.sunk | while | flops 563214336 | bytes 30480980 | solution.py:198
  171.2 4.4 fusion.167
  181.8 4.4 fusion.167
  192.3 4.4 fusion.167
  202.8 4.4 fusion.167
  213.3 4.4 fusion.167
  223.9 4.4 fusion.167
  234.4 4.4 fusion.167
  244.9 4.4 fusion.167
  249.5 6.3 fusion.116
  258.6 11.5 %copy.96 = bf16[2,8,512,512]{3,1,2,0:T(8,128)(2,1)} copy(bf16[2,8,512,512]{3,2,1,0:T(8,128)(2,1)} %bitcast.279) | data formatting | bytes 16777216 | tf_op jit(solution)/shard_map/reshape | solution.py:21
  270.1 12.6 %copy.120 = bf16[128,8,8,512]{3,1,2,0:T(8,128)(2,1)} copy(bf16[128,8,8,512]{3,2,1,0:T(8,128)(2,1)} %bitcast.269) | data formatting | bytes 16777216
  282.7 14.9 %copy.97 = bf16[2,8,512,512]{2,1,3,0:T(8,128)(2,1)} copy(bf16[2,8,512,512]{3,2,1,0:T(8,128)(2,1)} %bitcast.280) | data formatting | bytes 16777216 | tf_op jit(solution)/shard_map/reshape | solution.py:21
  297.6 12.2 %copy.121 = bf16[128,8,8,512]{3,1,2,0:T(8,128)(2,1)} copy(bf16[128,8,8,512]{3,2,1,0:T(8,128)(2,1)} %bitcast.270) | data formatting | bytes 16777216
  309.9 47.6 %fusion.60 = (bf16[1024,4096]{1,0:T(8,128)(2,1)}, f32[1024,4096]{1,0:T(8,128)}) fusion(f32[4096]{0:T(1024)S(1)} %bitcast.310, bf16[1024,4096]{1,0:T(8,128)(2,1)} %bitcast.281, bf16[1024,1024]{0,1:T(8,128)(2,1)S(1)} %fusion.108.clone.4), kind=kOutput, calls=%fused_computation.67 | convolution fusion | flops 8866758656 | bytes 35667968 | tf_op jit(solution)/shard_map/dot_general | solution.py:211
  357.6 11.6 %fusion.117 = (f32[1024]{0:T(1024)S(1)}, f32[1024,1024]{0,1:T(8,128)S(1)}) fusion(f32[1024]{0:T(1024)S(1)} %copy-done.54, bf16[1024,4096]{1,0:T(8,128)(2,1)} %get-tuple-element.278, bf16[4096,1024]{0,1:T(8,128)(2,1)S(1)} %bitcast.286, f32[1024]{0:T(1024)S(1)} %copy-done.47, f32[1024]{0:T(1024)S(1)} %copy-done.36, f32[1024]{0:T(1024)S(1)} %copy-done.31, ...), kind=kOutput, calls=%fused_computation.176 | convolution fusion | flops 8597273600 | bytes 25190400 | tf_op jit(solution)/shard_map/dot_general | solution.py:214
  373.4 23.7 %fusion.118 = (f32[4096]{0:T(1024)}, bf16[1024,4096]{1,0:T(8,128)(2,1)}) fusion(f32[1024,4096]{1,0:T(8,128)} %get-tuple-element.279, f32[4096]{0:T(1024)S(1)} %bitcast.311, bf16[4096,1024]{0,1:T(8,128)(2,1)} %bitcast.285, f32[1024]{0:T(1024)S(1)} %broadcast_multiply_fusion.2, f32[1024,1024]{0,1:T(8,128)S(1)} %get-tuple-element.281, ...), kind=kOutput, calls=%fused_computation.177 | convolution fusion | flops 8649699328 | bytes 39899136 | tf_op jit(solution)/shard_map/dot_general | solution.py:226
  397.1 15.3 %multiply_reduce_fusion.1 = (f32[1024]{0:T(1024)}, f32[1024]{0:T(1024)S(1)}, f32[1024]{0:T(1024)S(1)}, f32[1024]{0:T(1024)}, f32[1024,1024]{0,1:T(8,128)}) fusion(f32[1024,1024]{0,1:T(8,128)S(1)} %copy-done.3, f32[1024]{0:T(1024)S(1)} %copy-done.31, f32[1024]{0:T(1024)S(1)} %copy-done.25, f32[1024]{0:T(1024)S(1)} %copy-done.36, ...), kind=kOutput, calls=%fused_computation.108 | convolution fusion | flops 8608804864 | bytes 31506432 | tf_op jit(solution)/shard_map/dot_general | solution.py:238
  412.5 4.4 fusion.112
  419.3 5.3 convolution_convert_fusion.2
  424.6 154.8 %while.29 = (s32[]{:T(128)}, f32[8,1024,2,64]{1,3,2,0:T(8,128)}, bf16[8,1024,2,64]{1,3,2,0:T(8,128)(2,1)}, f32[8,1024,2,64]{1,3,2,0:T(8,128)}, bf16[8,1024,2,64]...) while((s32[]{:T(128)}, f32[8,1024,2,64]{1,3,2,0:T(8,128)}, ...), condition=%wide.region_14.15_spmd.clone, body=%wide.region_12.14_spmd.clone.sunk | while | flops 1374943232 | bytes 70583408 | solution.py:254
  428.5 3.9 multiply_reduce_fusion.7
  447.8 3.9 multiply_reduce_fusion.7
  467.1 3.9 multiply_reduce_fusion.7
  486.5 3.9 multiply_reduce_fusion.7
  505.8 3.9 multiply_reduce_fusion.7
  525.1 3.9 multiply_reduce_fusion.7
  544.4 3.9 multiply_reduce_fusion.7
  563.8 3.9 multiply_reduce_fusion.7
  582.3 3.7 convert_bitcast_fusion.2
  588.5 5.1 reshape.297
  597.0 5.2 convert_bitcast_fusion
  605.6 4.5 stack.36
  610.1 6.0 convert_bitcast_fusion.1
  616.1 4.5 stack.35
  620.6 12.8 %maximum_bitcast_fusion = bf16[2,8,3,512,128]{3,0,4,1,2:T(2,128)(2,1)} fusion(bf16[1,2,512,8,128]{2,1,4,3,0:T(2,128)(2,1)} %stack.36, bf16[1,2,512,8,128]{2,1,4,3,0:T(2,128)(2,1)} %stack.35, bf16[1,2,512,8,128]{2,1,4,3,0:T(2,128)(2,1)S(1)} %stack.34), kind=kLoop, calls=%fused_computation.91 | loop fusion | flops 6291456 | bytes 12582912 | tf_op jit(solution)/shard_map/transpose | solution.py:49
  633.4 16.2 %copy.104 = bf16[2,8,3,512,128]{4,3,2,1,0:T(8,128)(2,1)} copy(bf16[2,8,3,512,128]{3,0,4,1,2:T(2,128)(2,1)} %maximum_bitcast_fusion) | data formatting | bytes 12582912 | tf_op jit(solution)/shard_map/transpose | solution.py:49
  651.3 16.7 %convolution_convert_fusion = bf16[4096,1024]{1,0:T(8,128)(2,1)} fusion(bf16[1024,4096]{1,0:T(8,128)(2,1)} %get-tuple-element.278, bf16[1024,1024]{0,1:T(8,128)(2,1)S(1)} %copy-done.8, f32[1024,1024]{0,1:T(8,128)} %copy-done.4, f32[1024]{0:T(1024)S(1)} %copy-done.39, f32[1024]{0:T(1024)S(1)} %copy-done.41, f32[1024]{0:T(1024)S(1)} %copy-done.45, ...), kind=kOutput, calls=%fused_computation.89 | convolution fusion | flops 8603566080 | bytes 23089152 | tf_op jit(solution)/shard_map/dot_general | solution.py:222
  668.0 14.9 %reshape.301 = bf16[8,512,2,512]{3,2,1,0:T(2,128)(2,1)} reshape(bf16[4096,1024]{1,0:T(8,128)(2,1)} %convolution_convert_fusion) | data formatting | bytes 16777216 | tf_op jit(solution)/shard_map/reshape | solution.py:62
  682.9 8.7 copy.107
  692.3 15.5 %convolution_convert_fusion.1 = bf16[1024,4096]{1,0:T(8,128)(2,1)} fusion(bf16[1024,4096]{1,0:T(8,128)(2,1)} %get-tuple-element.284, f32[1024,1024]{0,1:T(8,128)} %copy-done.2, f32[1024]{0:T(1024)S(1)} %copy-done.48, f32[1024]{0:T(1024)S(1)} %copy-done.37, f32[1024]{0:T(1024)S(1)} %copy-done.32, f32[1024]{0:T(1024)S(1)} %copy-done.26), kind=kOutput, calls=%fused_computation.90 | convolution fusion | flops 8599371776 | bytes 20987904 | tf_op jit(solution)/shard_map/dot_general | solution.py:234
  707.8 12.2 %copy.125 = bf16[128,8,8,512]{3,2,1,0:T(8,128)(2,1)} copy(bf16[128,8,8,512]{3,1,2,0:T(8,128)(2,1)} %bitcast.287) | data formatting | bytes 16777216
  720.0 7.2 bitcast_bitcast_fusion
  727.3 9.9 copy.106
  742.5 5.3 fusion.79
  748.5 6.3 fusion.114
  757.9 4.5 fusion.119
  762.4 89.7 %reduce-scatter.11.cloned.1.call-done = bf16[1,512,512]{2,1,0:T(8,128)(2,1)} async-done(((bf16[16,512,512]{2,1,0:T(8,128)(2,1)}), bf16[1,512,512]{2,1,0:T(8,128)(2,1)}) %reduce-scatter.11.cloned.1.call-update) | async-done | bytes 524304 | tf_op jit(solution)/shard_map/reduce_scatter | solution.py:41
  852.1 107.2 %reduce-scatter.9.cloned.1.call-done = bf16[1,512,512]{2,1,0:T(8,128)(2,1)} async-done(((bf16[16,512,512]{2,1,0:T(8,128)(2,1)}), bf16[1,512,512]{2,1,0:T(8,128)(2,1)}) %reduce-scatter.9.cloned.1.call-update) | async-done | bytes 524304 | tf_op jit(solution)/shard_map/reduce_scatter | solution.py:41
  959.4 4.8 fusion.120
  964.7 5.0 add_add_fusion
  969.7 5.5 copy.109
  977.7 39.8 %all-gather.20.cloned.1.call-done = f32[393216]{0:T(1024)} async-done(((f32[12288]{0:T(1024)}), f32[393216]{0:T(1024)}) %all-gather.20.cloned.1.call-update) | async-done | bytes 1572880 | tf_op jit(solution)/shard_map/all_gather | solution.py:290
  1021.3 49.2 %all-reduce.3.cloned.1.call-done = (bf16[3,512,128]{2,1,0:T(8,128)(2,1)}, bf16[128,512]{1,0:T(8,128)(2,1)}, bf16[512,512]{1,0:T(8,128)(2,1)}, bf16[512,512]{1,0:T(8,128)(2,1)}) async-done(((bf16[3,512,128]{2,1,0:T(8,128)(2,1)}, bf16[128,512]{1,0:T(8,128)(2,1)}, bf16[512,512]{1,0:T(8,128)(2,1)}, bf16[512,512]{1,0:T(8,128)(2,1)}), (bf16[3,512,128]{2,1,0:T(8,128)(2,1)}, bf16[128,512]{1,0:T(8,128)(2,1)}, ...) | async-done | bytes 1572880 | tf_op jit(solution)/shard_map/psum | solution.py:42
  (283 shorter events, 230.4 us)
Async XLA Ops:
  7.2 36.1 %copy-start = (s32[8,1024]{1,0:T(8,128)S(1)}, s32[8,1024]{1,0:T(8,128)}, u32[]{:S(2)}) copy-start(s32[8,1024]{1,0:T(8,128)} %param.20) | copy-start | bytes 98308
  7.2 20.8 %copy-start.52 = (f32[512]{0:T(512)S(1)}, f32[512]{0:T(512)}, u32[]{:S(2)}) copy-start(f32[512]{0:T(512)} %param.28) | copy-start | bytes 6148
  7.2 33.5 %copy-start.18 = (bf16[1024,1024]{1,0:T(8,128)(2,1)S(1)}, bf16[1024,1024]{1,0:T(8,128)(2,1)}, u32[]{:S(2)}) copy-start(bf16[1024,1024]{1,0:T(8,128)(2,1)} %param.33) | copy-start | bytes 6291460
  7.2 47.2 %all-gather.14.cloned.1.call-start = ((), (), s32[]{:S(2)}) async-start(), calls=%async_computation.9 | async-start | bytes 2228224 | tf_op jit(solution)/shard_map/all_gather | solution.py:20
  8.0 109.0 %all-gather.12.cloned.1.call-start = ((), (), s32[]{:S(2)}) async-start(), calls=%async_computation.8 | async-start | bytes 6684672 | tf_op jit(solution)/shard_map/all_gather | solution.py:20
  8.7 249.9 %all-gather.16.cloned.1.call-start = ((), (), s32[]{:S(2)}) async-start(), calls=%async_computation.10 | async-start | bytes 8912896 | tf_op jit(solution)/shard_map/all_gather | solution.py:20
  9.4 273.3 %all-gather.18.cloned.1.call-start = ((), (), s32[]{:S(2)}) async-start(), calls=%async_computation.11 | async-start | bytes 8912896 | tf_op jit(solution)/shard_map/all_gather | solution.py:20
  10.0 752.4 %reduce-scatter.7.cloned.1.call-start = ((), (), s32[]{:S(2)}) async-start(), calls=%async_computation.5 | async-start | bytes 2228224 | tf_op jit(solution)/shard_map/reduce_scatter | solution.py:41
  153.8 4.5 copy-start.13
  165.1 84.4 %copy-start.53 = (f32[1024]{0:T(1024)S(1)}, f32[1024]{0:T(1024)}, u32[]{:S(2)}) copy-start(f32[1024]{0:T(1024)} %param.24) | copy-start | bytes 12292
  249.5 6.4 copy-start.11
  249.5 6.4 copy-start.21
  255.9 2.0 copy-start.2
  255.9 2.0 copy-start.35
  255.9 2.0 copy-start.46
  255.9 2.6 copy-start.24
  257.9 12.2 %copy-start.30 = (f32[1024]{0:T(1024)}, f32[1024]{0:T(1024)S(1)}, u32[]{:S(2)}) copy-start(f32[1024]{0:T(1024)S(1)} %add_rsqrt_fusion.1) | copy-start | bytes 12292
  309.8 47.7 %copy-start.3 = (f32[1024,1024]{0,1:T(8,128)S(1)}, f32[1024,1024]{0,1:T(8,128)}, u32[]{:S(2)}) copy-start(f32[1024,1024]{0,1:T(8,128)} %copy-done.2) | copy-start | bytes 12582916
  309.8 47.7 %copy-start.14 = (bf16[128,8,8,512]{3,1,2,0:T(8,128)(2,1)S(1)}, bf16[128,8,8,512]{3,1,2,0:T(8,128)(2,1)}, u32[]{:S(2)}) copy-start(bf16[128,8,8,512]{3,1,2,0:T(8,128)(2,1)} %copy.121) | copy-start | bytes 25165828
  309.8 47.7 %copy-start.25 = (f32[1024]{0:T(1024)S(1)}, f32[1024]{0:T(1024)}, u32[]{:S(2)}) copy-start(f32[1024]{0:T(1024)} %copy-done.24) | copy-start | bytes 12292
  309.8 47.7 %copy-start.31 = (f32[1024]{0:T(1024)S(1)}, f32[1024]{0:T(1024)}, u32[]{:S(2)}) copy-start(f32[1024]{0:T(1024)} %copy-done.30) | copy-start | bytes 12292
  309.8 47.7 %copy-start.36 = (f32[1024]{0:T(1024)S(1)}, f32[1024]{0:T(1024)}, u32[]{:S(2)}) copy-start(f32[1024]{0:T(1024)} %param.25) | copy-start | bytes 12292
  309.8 47.7 %copy-start.47 = (f32[1024]{0:T(1024)S(1)}, f32[1024]{0:T(1024)}, u32[]{:S(2)}) copy-start(f32[1024]{0:T(1024)} %param.26) | copy-start | bytes 12292
  309.9 47.7 %copy-start.54 = (f32[1024]{0:T(1024)S(1)}, f32[1024]{0:T(1024)}, u32[]{:S(2)}) copy-start(f32[1024]{0:T(1024)} %param.30) | copy-start | bytes 12292
  369.2 27.9 %copy-start.4 = (f32[1024,1024]{0,1:T(8,128)}, f32[1024,1024]{0,1:T(8,128)S(1)}, u32[]{:S(2)}) copy-start(f32[1024,1024]{0,1:T(8,128)S(1)} %get-tuple-element.281) | copy-start | bytes 12582916
  369.2 3.1 copy-start.7
  369.2 3.1 copy-start.44
  369.2 27.8 %copy-start.27 = (f32[1024]{0:T(1024)}, f32[1024]{0:T(1024)S(1)}, u32[]{:S(2)}) copy-start(f32[1024]{0:T(1024)S(1)} %broadcast_multiply_fusion.4) | copy-start | bytes 12292
  372.3 24.8 %copy-start.33 = (f32[1024]{0:T(1024)}, f32[1024]{0:T(1024)S(1)}, u32[]{:S(2)}) copy-start(f32[1024]{0:T(1024)S(1)} %add_rsqrt_fusion) | copy-start | bytes 12292
  372.3 24.8 %slice-start = ((s8[8388608]{0:T(1024)(128)(4,1)}), s8[4194304]{0:T(1024)(128)(4,1)S(1)}, s32[]{:S(2)}) async-start(s8[8388608]{0:T(1024)(128)(4,1)} %bitcast.282), calls=%async_computation.14 | async-start | bytes 8388608
  373.3 23.7 %copy-start.38 = (f32[1024]{0:T(1024)}, f32[1024]{0:T(1024)S(1)}, u32[]{:S(2)}) copy-start(f32[1024]{0:T(1024)S(1)} %broadcast_multiply_fusion.2) | copy-start | bytes 12292
  373.4 23.7 %copy-start.40 = (f32[1024]{0:T(1024)}, f32[1024]{0:T(1024)S(1)}, u32[]{:S(2)}) copy-start(f32[1024]{0:T(1024)S(1)} %broadcast_multiply_fusion.3) | copy-start | bytes 12292
  373.4 23.7 %slice-start.1 = ((s8[8388608]{0:T(1024)(128)(4,1)}), s8[4194304]{0:T(1024)(128)(4,1)S(1)}, s32[]{:S(2)}) async-start(s8[8388608]{0:T(1024)(128)(4,1)} %bitcast.282), calls=%async_computation.15 | async-start | bytes 8388608
  412.5 4.4 copy-start.20
  416.8 2.4 copy-start.5
  419.3 5.3 copy-start.22
  579.4 2.9 copy-start.19
  582.1 3.9 copy-start.16
  588.5 8.5 copy-start.9
  597.0 165.4 %reduce-scatter.5.cloned.1.call-start = ((), (), s32[]{:S(2)}) async-start(), calls=%async_computation.4 | async-start | bytes 6684672 | tf_op jit(solution)/shard_map/reduce_scatter | solution.py:41
  649.7 1.6 copy-start.8
  649.7 1.6 copy-start.28
  649.7 1.6 copy-start.34
  649.7 1.6 copy-start.39
  649.7 1.6 copy-start.41
  649.7 1.6 copy-start.45
  649.7 202.4 %reduce-scatter.11.cloned.1.call-start = ((), (), s32[]{:S(2)}) async-start(), calls=%async_computation.7 | async-start | bytes 8912896 | tf_op jit(solution)/shard_map/reduce_scatter | solution.py:41
  691.6 0.7 copy-start.37
  691.6 0.7 copy-start.48
  691.6 267.7 %reduce-scatter.9.cloned.1.call-start = ((), (), s32[]{:S(2)}) async-start(), calls=%async_computation.6 | async-start | bytes 8912896 | tf_op jit(solution)/shard_map/reduce_scatter | solution.py:41
  737.2 5.3 copy-start.43
  737.2 5.3 copy-start.42
  737.2 5.3 copy-start.51
  737.2 5.3 copy-start.50
  737.2 5.3 copy-start.49
  737.2 280.3 %all-gather.20.cloned.1.call-start = ((), (), s32[]{:S(2)}) async-start(), calls=%async_computation.12 | async-start | bytes 1622016 | tf_op jit(solution)/shard_map/all_gather | solution.py:290
  748.5 321.9 %all-reduce.3.cloned.1.call-start = ((), (), s32[]{:S(2)}) async-start(), calls=%async_computation.13 | async-start | bytes 3145728 | tf_op jit(solution)/shard_map/psum | solution.py:42
  755.4 2.5 copy-start.17
  959.3 4.9 copy-start.6
  959.3 4.9 copy-start.10
  959.3 5.3 copy-start.12
  969.7 5.5 copy-start.15
  975.2 102.2 %copy-start.1 = (s32[8,1024]{1,0:T(8,128)S(1)}, s32[8,1024]{1,0:T(8,128)}, u32[]{:S(2)}) copy-start(s32[8,1024]{1,0:T(8,128)} %param.20) | copy-start | bytes 98308
  1070.4 6.3 copy-start.23
  (3 other events, 2.0 us)
Sparse Core Ops, SparseCore 0:
  10.2 44.1 all-gather.13
  56.8 60.1 all-gather.11
  119.1 72.9 all-gather.15
  194.2 72.9 all-gather.17
  597.1 60.4 reduce-scatter.6
  661.3 84.0 reduce-scatter.4
  749.5 102.5 reduce-scatter.10
  856.2 103.0 reduce-scatter.8
  962.9 54.6 all-gather.19
  1019.9 50.4 all-reduce.2

commit v2 on v1

v2 whole, which is shorter than its diff:
```python
import jax
import jax.numpy as jnp
from jax import lax
from jax.experimental.layout import Layout, with_layout_constraint
from jax.experimental import pallas as pl
from jax.experimental.pallas import tpu as pltpu
from jax.sharding import PartitionSpec as P


import math

HEAD_DIM = 64
LEN = 1024
BLOCK = 256
PAIR = 128
FAR = 1e15
SCALE = HEAD_DIM ** (-0.5)
EPSILON = 1e-05
OWNERS = ("shard", "tensor")
EVERYONE = ("replica", "shard", "tensor")


def lanes_of(head, rows):
    lane = lax.broadcasted_iota(jnp.int32, (rows, PAIR), 1)
    return (lane // HEAD_DIM) == head


def with_marks(rows_block, marks, head):
    return jnp.where(lanes_of(head, rows_block.shape[0]), rows_block, marks)


def only_head(rows_block, head):
    return jnp.where(lanes_of(head, rows_block.shape[0]), rows_block, jnp.zeros_like(rows_block))


def attend_kernel(bounds, q_ref, k_ref, v_ref, qmark_ref, kmark_ref, o_ref, lse_ref):
    s_id = pl.program_id(0)
    blocks = q_ref.shape[0] // BLOCK
    for qb in range(blocks):
        rows = slice(qb * BLOCK, (qb + 1) * BLOCK)
        q = q_ref[rows, :]
        qmark = qmark_ref[rows, :]
        q_aug = [with_marks(q, qmark, h) for h in range(2)]

        def step(kb, carry):
            keys = pl.ds(pl.multiple_of(kb * BLOCK, BLOCK), BLOCK)
            k = k_ref[keys, :]
            v = v_ref[keys, :]
            kmark = kmark_ref[keys, :]
            out = []
            for h in range(2):
                top, total, acc = carry[h]
                scores = lax.dot_general(q_aug[h], with_marks(k, kmark, h), (((1,), (1,)), ((), ())),
                                         preferred_element_type=jnp.float32)
                new_top = jnp.maximum(top, jnp.max(scores, axis=-1, keepdims=True))
                fade = jnp.exp(top - new_top)
                weights = jnp.exp(scores - new_top)
                total = total * fade + jnp.sum(weights, axis=-1, keepdims=True)
                acc = acc * fade + jnp.dot(weights.astype(jnp.bfloat16), v, preferred_element_type=jnp.float32)
                out.append((new_top, total, acc))
            return tuple(out)

        start = tuple((jnp.full((BLOCK, 1), -3e38, jnp.float32), jnp.zeros((BLOCK, 1), jnp.float32),
                       jnp.zeros((BLOCK, PAIR), jnp.float32)) for _ in range(2))
        done = lax.fori_loop(bounds[s_id, 0, qb], bounds[s_id, 1, qb], step, start)
        (m0, l0, a0), (m1, l1, a1) = done
        o_ref[rows, :] = jnp.where(lanes_of(0, BLOCK), a0 / l0, a1 / l1).astype(o_ref.dtype)
        lse = jnp.where(lanes_of(0, BLOCK), m0 + jnp.log(l0), m1 + jnp.log(l1))
        flat = jnp.transpose(lse)
        lse_ref[0:1, rows] = flat[0:1, :]
        lse_ref[1:2, rows] = flat[HEAD_DIM:HEAD_DIM + 1, :]


def attend_back_kernel(bounds, q_ref, k_ref, v_ref, qmark_ref, kmark_ref, lse_ref, o_ref, do_ref,
                       dq_ref, dk_ref, dv_ref, dq_acc, delta_acc):
    s_id = pl.program_id(0)
    q_blocks = q_ref.shape[0] // BLOCK
    dq_acc[...] = jnp.zeros_like(dq_acc)
    for qb in range(q_blocks):
        rows = slice(qb * BLOCK, (qb + 1) * BLOCK)
        prod = do_ref[rows, :].astype(jnp.float32) * o_ref[rows, :].astype(jnp.float32)
        flat = jnp.transpose(prod)
        delta_acc[0:1, rows] = jnp.sum(flat[:HEAD_DIM, :], axis=0, keepdims=True)
        delta_acc[1:2, rows] = jnp.sum(flat[HEAD_DIM:, :], axis=0, keepdims=True)
    for kb in range(k_ref.shape[0] // BLOCK):
        keys = slice(kb * BLOCK, (kb + 1) * BLOCK)
        k = k_ref[keys, :]
        v = v_ref[keys, :]
        kmark = kmark_ref[keys, :]
        k_aug = [with_marks(k, kmark, h) for h in range(2)]
        v_own = [only_head(v, h) for h in range(2)]

        def step(qb, carry):
            rows = pl.ds(pl.multiple_of(qb * BLOCK, BLOCK), BLOCK)
            q = q_ref[rows, :]
            do = do_ref[rows, :]
            qmark = qmark_ref[rows, :]
            out, dq_parts = [], []
            for h in range(2):
                dk, dv = carry[h]
                scores = lax.dot_general(k_aug[h], with_marks(q, qmark, h), (((1,), (1,)), ((), ())),
                                         preferred_element_type=jnp.float32)
                probs = jnp.exp(scores - lse_ref[h:h + 1, rows])
                prob_grad = lax.dot_general(v_own[h], do, (((1,), (1,)), ((), ())),
                                            preferred_element_type=jnp.float32)
                score_low = (probs * (prob_grad - delta_acc[h:h + 1, rows])).astype(jnp.bfloat16)
                dv = dv + jnp.dot(probs.astype(jnp.bfloat16), do, preferred_element_type=jnp.float32)
                dk = dk + jnp.dot(score_low, q, preferred_element_type=jnp.float32)
                dq_parts.append(lax.dot_general(score_low, k, (((0,), (0,)), ((), ())),
                                                preferred_element_type=jnp.float32))
                out.append((dk, dv))
            dq_acc[rows, :] += jnp.where(lanes_of(0, BLOCK), dq_parts[0], dq_parts[1])
            return tuple(out)

        zero = jnp.zeros((BLOCK, PAIR), jnp.float32)
        done = lax.fori_loop(bounds[s_id, 2, kb], bounds[s_id, 3, kb], step, ((zero, zero), (zero, zero)))
        dk_ref[keys, :] = jnp.where(lanes_of(0, BLOCK), done[0][0], done[1][0]).astype(dk_ref.dtype)
        dv_ref[keys, :] = jnp.where(lanes_of(0, BLOCK), done[0][1], done[1][1]).astype(dv_ref.dtype)
    dq_ref[...] = (dq_acc[...] * SCALE).astype(dq_ref.dtype)


def block_bounds(q_seg, k_seg):
    def ranges(mine, other):
        first = mine[:, ::BLOCK][:, :, None]
        last = mine[:, BLOCK - 1::BLOCK][:, :, None]
        low = jnp.sum((other[:, None, :] < first).astype(jnp.int32), axis=-1) // BLOCK
        high = (jnp.sum((other[:, None, :] <= last).astype(jnp.int32), axis=-1) + BLOCK - 1) // BLOCK
        return low, jnp.maximum(high, low)

    wide = k_seg.shape[1] // BLOCK

    def pad(table):
        return jnp.pad(table, ((0, 0), (0, wide - table.shape[1])))

    kl, kh = ranges(q_seg, k_seg)
    ql, qh = ranges(k_seg, q_seg)
    return jnp.stack([pad(kl), pad(kh), pad(ql), pad(qh)], axis=1)


def doc_marks(segments, far):
    lane = lax.broadcasted_iota(jnp.int32, segments.shape + (PAIR,), segments.ndim) % HEAD_DIM
    own = lane == segments[..., None]
    docs = lane < 4
    if far:
        return jnp.where(docs & ~own, -FAR, 0.0).astype(jnp.bfloat16)
    return jnp.where(own, FAR, 0.0).astype(jnp.bfloat16)


def specs(rows):
    own = pl.BlockSpec((None, rows, PAIR), lambda s, p, b: (p, s, 0))
    shared = pl.BlockSpec((None, rows, PAIR), lambda s, p, b: (s, 0, 0))
    return own, shared


def attend(q, k, v, q_mark, k_mark, bounds):
    pairs, seqs = q.shape[0], q_mark.shape[0]
    rows = q.shape[1] // seqs
    q_spec, qm_spec = specs(rows)
    k_spec, km_spec = specs(LEN)
    lse_spec = pl.BlockSpec((None, None, 2, rows), lambda s, p, b: (s, p, 0, 0))
    return pl.pallas_call(
        attend_kernel,
        grid_spec=pltpu.PrefetchScalarGridSpec(
            num_scalar_prefetch=1,
            grid=(seqs, pairs),
            in_specs=[q_spec, k_spec, k_spec, qm_spec, km_spec],
            out_specs=[q_spec, lse_spec],
        ),
        out_shape=[
            jax.ShapeDtypeStruct(q.shape, jnp.bfloat16),
            jax.ShapeDtypeStruct((seqs, pairs, 2, rows), jnp.float32),
        ],
        cost_estimate=pl.CostEstimate(
            flops=8 * q.size * LEN, bytes_accessed=12 * k.size, transcendentals=2 * rows * LEN * pairs
        ),
        name="attend",
    )(bounds, q, k, v, q_mark, k_mark)


def attend_back(q, k, v, q_mark, k_mark, bounds, lse, o, do, kv_type):
    pairs, seqs = q.shape[0], q_mark.shape[0]
    rows = q.shape[1] // seqs
    q_spec, qm_spec = specs(rows)
    k_spec, km_spec = specs(LEN)
    lse_spec = pl.BlockSpec((None, None, 2, rows), lambda s, p, b: (s, p, 0, 0))
    return pl.pallas_call(
        attend_back_kernel,
        grid_spec=pltpu.PrefetchScalarGridSpec(
            num_scalar_prefetch=1,
            grid=(seqs, pairs),
            in_specs=[q_spec, k_spec, k_spec, qm_spec, km_spec, lse_spec, q_spec, q_spec],
            out_specs=[q_spec, k_spec, k_spec],
            scratch_shapes=[pltpu.VMEM((rows, PAIR), jnp.float32), pltpu.VMEM((2, rows), jnp.float32)],
        ),
        out_shape=[
            jax.ShapeDtypeStruct(q.shape, kv_type),
            jax.ShapeDtypeStruct(k.shape, kv_type),
            jax.ShapeDtypeStruct(k.shape, kv_type),
        ],
        cost_estimate=pl.CostEstimate(
            flops=20 * q.size * LEN, bytes_accessed=24 * k.size, transcendentals=2 * rows * LEN * pairs
        ),
        name="attend_back",
    )(bounds, q, k, v, q_mark, k_mark, lse, o, do)


def gather_blocks(weight):
    blocks = lax.all_gather(weight, OWNERS, axis=0, tiled=False)
    return blocks.reshape((lax.axis_size("shard"), lax.axis_size("tensor")) + weight.shape)


def pair_blocks(blocks):
    shards, _, three, rows, cols = blocks.shape
    if cols == PAIR:
        return blocks
    columns = blocks.transpose(0, 2, 3, 1, 4).reshape(shards, three, rows, -1, PAIR)
    return columns.transpose(0, 3, 1, 2, 4)


def unpair_blocks(blocks, tensors):
    shards, pairs, four, _, rows = blocks.shape
    if pairs == tensors:
        return blocks
    split = blocks.reshape(shards, pairs, four, tensors // pairs, -1, rows)
    return split.transpose(0, 1, 3, 2, 4, 5)


def scatter_blocks(blocks, block_shape):
    flat = blocks.reshape(-1, block_shape[-1])
    flat = with_layout_constraint(flat, Layout(major_to_minor=(0, 1)))
    owned = lax.psum_scatter(flat, OWNERS, scatter_dimension=0, tiled=True)
    owned = with_layout_constraint(owned, Layout(major_to_minor=(0, 1)))
    return owned.reshape(block_shape)


def over_replicas(owned):
    count = lax.axis_size("replica")
    total = owned.astype(jnp.float32)
    for step in range(1, count):
        ring = [(i, (i + step) % count) for i in range(count)]
        total = total + lax.ppermute(owned, "replica", ring).astype(jnp.float32)
    return total


def sum_over(values, axis):
    count = lax.axis_size(axis)
    if count & (count - 1):
        return lax.psum(values, axis)
    step = 1
    while step < count:
        values = values + lax.ppermute(values, axis, [(i, i ^ step) for i in range(count)])
        step *= 2
    return values


def dot(spec, left, right):
    return jnp.einsum(spec, left, right, preferred_element_type=jnp.float32)


def mean_of(values):
    return jnp.mean(values, axis=(0, 2), keepdims=True)


def normalize(residual, gain_vec, shift_vec):
    center = residual - mean_of(residual)
    spread = lax.rsqrt(mean_of(center * center) + EPSILON)
    normed = center * spread
    return (normed * gain_vec + shift_vec, normed, spread)


def norm_back(incoming, normed, spread, gain_vec):
    scaled = incoming * gain_vec
    back_grad = spread * (scaled - mean_of(scaled) - normed * mean_of(scaled * normed))
    return (back_grad, jnp.sum(incoming * normed, axis=1), jnp.sum(incoming, axis=1))


def layer(
    layer_input,
    segment_ids,
    qkv_weight,
    qkv_bias,
    out_weight,
    out_bias,
    norm1_gain,
    norm1_bias,
    up_weight,
    up_bias,
    down_weight,
    down_bias,
    norm2_gain,
    norm2_bias,
    output_grad,
):
    rows, width = layer_input.shape
    tensor_index = lax.axis_index("tensor")
    tensors = lax.axis_size("tensor")
    shards = lax.axis_size("shard")
    pairs = width // PAIR
    sharers = max(1, LEN // rows)
    seqs_here = max(1, rows // LEN)
    query_rows = min(rows, LEN)
    sharing = [list(range(i, i + sharers)) for i in range(0, tensors, sharers)]

    w_attn = gather_blocks(jnp.concatenate([qkv_weight, out_weight.T[None]]))
    w_up = gather_blocks(up_weight)
    w_down = gather_blocks(down_weight)
    w_attn = pair_blocks(w_attn)
    w_qkv, w_out = w_attn[:, :, :3], w_attn[:, :, 3]
    biases = lax.all_gather(
        jnp.concatenate([qkv_bias[0], qkv_bias[1], up_bias]), "tensor", axis=0, tiled=False
    )
    width_here, hidden_here = qkv_bias.shape[1], up_bias.shape[0]
    bias_q = biases[:, :width_here].reshape(pairs, 1, PAIR)
    bias_v = biases[:, width_here : 2 * width_here].reshape(pairs, 1, PAIR)
    bias_up = biases[:, 2 * width_here :].reshape(tensors, 1, hidden_here)

    def vec(values):
        return values.reshape(shards, 1, width // shards)

    def halves(rows_array):
        return rows_array.reshape(rows, shards, width // shards).transpose(1, 0, 2)

    def whole(blocks):
        return blocks.transpose(1, 0, 2).reshape(rows, width)

    first_seq = tensor_index * rows // LEN
    key_segments = lax.dynamic_slice_in_dim(segment_ids, first_seq, seqs_here, 0)
    query_start = tensor_index * rows % LEN
    query_segments = lax.dynamic_slice_in_dim(key_segments, query_start, query_rows, 1)
    bounds = block_bounds(query_segments, key_segments)
    q_mark, k_mark = doc_marks(query_segments, True), doc_marks(key_segments, False)

    def whole_rows(rows_array):
        if sharers == 1:
            return rows_array
        return lax.all_gather(rows_array, "tensor", axis_index_groups=sharing, axis=1, tiled=True)

    def own_rows(rows_array):
        if sharers == 1:
            return rows_array
        return lax.psum_scatter(
            rows_array, "tensor", axis_index_groups=sharing, scatter_dimension=1, tiled=True
        )

    tokens = halves(layer_input)
    projected = dot("std,snjdc->jntc", tokens, w_qkv)
    queries = ((projected[0] + bias_q).astype(jnp.bfloat16) * SCALE).astype(jnp.bfloat16)
    key_rows = whole_rows(projected[1].astype(jnp.bfloat16))
    value_rows = whole_rows((projected[2] + bias_v).astype(jnp.bfloat16))
    mixed, log_total = attend(queries, key_rows, value_rows, q_mark, k_mark, bounds)
    residual_one = tokens.astype(jnp.float32) + dot("ntc,sndc->std", mixed, w_out) + vec(out_bias)
    hidden_one, normed_one, spread_one = normalize(residual_one, vec(norm1_gain), vec(norm1_bias))
    hidden_low = hidden_one.astype(jnp.bfloat16)
    pre_act = dot("std,sndf->ntf", hidden_low, w_up) + bias_up
    normal_cdf = 0.5 * (1.0 + lax.erf(pre_act * (1.0 / math.sqrt(2.0))))
    normal_pdf = jnp.exp(-0.5 * pre_act * pre_act) * (1.0 / math.sqrt(2.0 * math.pi))
    activ = (pre_act * normal_cdf).astype(jnp.bfloat16)
    slope = (normal_cdf + pre_act * normal_pdf).astype(jnp.bfloat16)
    activ, slope = lax.optimization_barrier((activ, slope))
    residual_two = hidden_one + dot("ntf,snfd->std", activ, w_down) + vec(down_bias)
    final_out, normed_two, spread_two = normalize(residual_two, vec(norm2_gain), vec(norm2_bias))
    resid_two_grad, gain_two_grad, shift_two_grad = norm_back(
        halves(output_grad).astype(jnp.float32), normed_two, spread_two, vec(norm2_gain)
    )
    down_bias_part = jnp.sum(resid_two_grad, axis=1)
    branch_grad = resid_two_grad.astype(jnp.bfloat16)
    down_grad = dot("ntf,std->sndf", activ, branch_grad).astype(jnp.bfloat16)
    down_owned = scatter_blocks(down_grad, down_weight.shape[::-1])
    activ_grad = dot("std,snfd->ntf", branch_grad, w_down)
    pre_grad = activ_grad * slope.astype(jnp.float32)
    up_bias_part = jnp.sum(pre_grad, axis=1)
    pre_low = pre_grad.astype(jnp.bfloat16)
    up_grad = dot("ntf,std->sndf", pre_low, hidden_low).astype(jnp.bfloat16)
    up_owned = scatter_blocks(up_grad, up_weight.shape)
    back_middle = dot("ntf,sndf->std", pre_low, w_up)
    resid_one_grad, gain_one_grad, shift_one_grad = norm_back(
        resid_two_grad + back_middle, normed_one, spread_one, vec(norm1_gain)
    )
    out_bias_part = jnp.sum(resid_one_grad, axis=1)
    attn_grad = resid_one_grad.astype(jnp.bfloat16)
    out_grad = dot("ntc,std->sncd", mixed, attn_grad).astype(jnp.bfloat16)
    mixed_grad = dot("std,sndc->ntc", attn_grad, w_out).astype(jnp.bfloat16)
    grad_type = jnp.bfloat16 if sharers == 1 else jnp.float32
    query_grad, key_grad, value_grad = attend_back(
        queries, key_rows, value_rows, q_mark, k_mark, bounds, log_total, mixed, mixed_grad, grad_type
    )
    key_grad, value_grad = own_rows(key_grad), own_rows(value_grad)
    proj_low = jnp.stack([query_grad, key_grad, value_grad]).astype(jnp.bfloat16)
    qkv_grad = [dot("ntc,std->sncd", proj_low[j], tokens).astype(jnp.bfloat16) for j in range(3)]
    attn_weight_grad = jnp.stack(qkv_grad + [out_grad], axis=2)
    attn_owned = scatter_blocks(
        unpair_blocks(attn_weight_grad, tensors), (4,) + out_weight.shape
    )
    back_input = dot("jntc,snjdc->std", proj_low, w_qkv)
    input_grad = resid_one_grad + back_input
    down_owned = over_replicas(down_owned).T
    up_owned = over_replicas(up_owned)
    attn_owned = over_replicas(attn_owned)
    qkv_owned, out_owned = attn_owned[:3].transpose(0, 2, 1), attn_owned[3]
    parts = (
        jnp.sum(query_grad.astype(jnp.float32), axis=1),
        jnp.sum(value_grad.astype(jnp.float32), axis=1),
        up_bias_part,
        out_bias_part,
        gain_one_grad,
        shift_one_grad,
        down_bias_part,
        gain_two_grad,
        shift_two_grad,
    )
    parts = [part.reshape(-1) for part in parts]
    summed = jnp.concatenate(parts).reshape(-1, PAIR)
    for axis in EVERYONE:
        summed = sum_over(summed, axis)
    summed = summed.reshape(-1)
    ends = [0]
    for part in parts:
        ends.append(ends[-1] + part.shape[0])
    summed = [summed[ends[i] : ends[i + 1]] for i in range(len(parts))]
    qkv_bias_grad = lax.dynamic_slice_in_dim(
        jnp.stack(summed[:2]), tensor_index * width_here, width_here, 1
    )
    up_bias_grad = lax.dynamic_slice_in_dim(summed[2], tensor_index * hidden_here, hidden_here, 0)
    return (
        whole(final_out.astype(jnp.bfloat16)),
        whole(input_grad),
        qkv_owned,
        qkv_bias_grad,
        out_owned,
        summed[3],
        summed[4],
        summed[5],
        up_owned,
        up_bias_grad,
        down_owned,
        summed[6],
        summed[7],
        summed[8],
    )


def solution(mesh):
    placed = (
        P(("replica", "shard", "tensor"), None),
        P(("replica", "shard"), None),
        P(None, "shard", "tensor"),
        P(None, "tensor"),
        P("tensor", "shard"),
        P(),
        P(),
        P(),
        P("shard", "tensor"),
        P("tensor"),
        P("tensor", "shard"),
        P(),
        P(),
        P(),
        P(("replica", "shard", "tensor"), None),
    )
    return jax.shard_map(
        layer,
        mesh=mesh,
        in_specs=placed,
        out_specs=(
            P(("replica", "shard", "tensor"), None),
            P(("replica", "shard", "tensor"), None),
            P(None, "shard", "tensor"),
            P(None, "tensor"),
            P("tensor", "shard"),
            P(),
            P(),
            P(),
            P("shard", "tensor"),
            P("tensor"),
            P("tensor", "shard"),
            P(),
            P(),
            P(),
        ),
        check_vma=False,
    )
```

time: 1100 us -> 684 us (0.62)
  matrix products: 363 us -> 163 us
  local copies, waits for them, and re-layouts: 222 us -> 35.3 us
  Pallas kernels: 0 us -> 122 us
  waiting for transfers between devices: 358 us -> 247 us
  other arithmetic: 98.6 us -> 39.2 us
  starting transfers between devices: 0.4 us -> 37.3 us
    dot_general x72 -> x14, matrix products: 363 us -> 163 us  [dot(): return jnp.einsum(spec, left, right, preferred_element_type=jnp.float32)]
    pallas_call x0 -> x2, Pallas kernels: none -> 122 us  [the longest x1 63 us: attend_back(): pl.pallas_call(attend_back_kernel, grid_spec=pltpu.PrefetchScalarGridSpec...]
    reshape x7 -> x0, local copies, waits for them, and re-layouts: 77.9 us -> none  [the longest x4 46.9 us: gather_blocks(): blocks.reshape((lax.axis_size('shard'), lax.axis_size('tensor')) + weight...]
    reduce_scatter x4 -> x3, waiting for transfers between devices: 197 us -> 137 us  [scatter_blocks(): owned = lax.psum_scatter(flat, OWNERS, scatter_dimension=0, tiled=True)]
    psum x1 -> x0, waiting for transfers between devices: 49.2 us -> none  [scatter_blocks(): return lax.psum(owned, 'replica').astype(jnp.float32)]
    unnamed x132 -> x109, local copies, waits for them, and re-layouts: 66.8 us -> 19.6 us
    transpose x5 -> x1, local copies, waits for them, and re-layouts: 45.3 us -> 0.05 us  [layer(): qkv_owned, out_owned = (attn_owned[:3].transpose(0, 2, 1), attn_owned[3])]
    all_gather x1 -> x0, waiting for transfers between devices: 39.8 us -> none  [body(): lax.all_gather(jnp.concatenate(parts), EVERYONE, axis=0, tiled=False)]
  transfers between devices with their start and end apart: 10 -> 14, of which waited for: 6 -> 8; matrix products, arithmetic and copies ran while one was open for 33% -> 28% of each run, Pallas kernels for 0% -> 18%
where the time goes in v2:
time: 684 us; the launch traced here: 674 us
  waiting for transfers between devices  247 us (36%)
  matrix products  163 us (24%)
  Pallas kernels  122 us (18%)
  other arithmetic  39.2 us (6%)
  starting transfers between devices  37.3 us (5%)
  local copies, waits for them, and re-layouts  35.3 us (5%)
  blocking collectives  15.9 us (2%)
  between operations  15.3 us (2%)
    dot_general x14, matrix products, dot(): return jnp.einsum(spec, left, right, preferred_element_type=jnp.float32)  163 us
    reduce_scatter x3, waiting for transfers between devices, scatter_blocks(): owned = lax.psum_scatter(flat, OWNERS, scatter_dimension=0, tiled=True)  137 us
    all_gather x3, waiting for transfers between devices, gather_blocks(): blocks = lax.all_gather(weight, OWNERS, axis=0, tiled=False)  95.4 us
    pallas_call x1, Pallas kernels, attend_back(): pl.pallas_call(attend_back_kernel, grid_spec=pltpu.PrefetchScalarGridSpec...  63 us
    pallas_call x1, Pallas kernels, attend(): pl.pallas_call(attend_kernel, grid_spec=pltpu.PrefetchScalarGridSpec(num_...  58.9 us
    ppermute x5, starting transfers between devices, sum_over(): lax.ppermute(values, axis, [(i, i ^ step) for i in range(count)])  32.1 us
    unnamed x109, local copies, waits for them, and re-layouts  19.6 us
    all_gather x1, blocking collectives, layer(): lax.all_gather(jnp.concatenate([qkv_bias[0], qkv_bias[1], up_bias]), 'ten...  15.9 us
  transfers between devices with their start and end apart: 14, of which 8 were waited for; matrix products, arithmetic and copies ran while one was open for 28% of the time, Pallas kernels for 18%

profile of v2, /device:TPU:0, one launch (start us, length us, event | category | flops | bytes accessed | tf_op | source)
XLA Modules:
  0.0 674.3 jit_solution(10901338714037890739)
XLA Ops:
  7.3 1.0 copy.117
  8.3 1.8 pad_maximum_fusion.1
  10.2 0.7 all-gather.11.cloned.1.call-update
  11.0 0.7 all-gather.13.cloned.1.call-update
  12.0 2.9 copy.116
  14.9 15.9 %all-gather.4 = f32[8,1,768]{2,1,0:T(1,128)S(1)} all-gather(f32[1,1,768]{2,1,0:T(1,128)S(1)} %reshape.792), channel_id=3, replica_groups=mesh['replica'=2,'shard'=2,'tensor'=8] {'tensor'}, dimensions={0}, use_global_device_ids=true | all-gather | bytes 27648 | tf_op jit(solution)/shard_map/all_gather | solution.py:309
  30.9 4.1 copy.125
  35.9 1.0 fusion.83
  36.9 51.1 %all-gather.9.cloned.1.call-done = bf16[64,512,128]{2,1,0:T(8,128)(2,1)} async-done(((bf16[4,512,128]{2,1,0:T(8,128)(2,1)}), bf16[64,512,128]{2,1,0:T(8,128)(2,1)}) %all-gather.9.cloned.1.call-update) | async-done | bytes 8388624 | tf_op jit(solution)/shard_map/all_gather | solution.py:208
  88.0 9.2 %fusion.24 = f32[3,8,1024,128]{3,2,1,0:T(8,128)S(1)} fusion(bf16[2,1024,512,1,1]{1,2,0,3,4:T(8,128)(2,1)S(1)} %bitcast.372, bf16[2,8,4,512,128]{4,3,2,1,0:T(8,128)(2,1)} %bitcast.409), kind=kOutput, calls=%fused_computation.30 | convolution fusion | flops 6442450944 | bytes 20971520 | tf_op jit(solution)/shard_map/std,snjdc->jntc/dot_general | solution.py:257
  97.2 1.7 fusion.48.k_ref
  98.9 1.7 fusion.28.v_ref
  100.6 1.7 fusion.47.q_ref
  102.3 58.9 %attend.1 = (bf16[8,1024,128]{2,1,0:T(8,128)(2,1)}, f32[1,8,2,1024]{3,2,1,0:T(2,128)}) custom-call(s32[1,4,4]{2,1,0:T(4,128)} %pad_add_fusion.bounds, bf16[8,1024,128]{2,1,0:T(8,128)(2,1)} %fusion.47.q_ref, bf16[8,1024,128]{2,1,0:T(8,128)(2,1)} %fusion.48.k_ref, bf16[8,1024,128]{2,1,0:T(8,128)(2,1)} %fusion.28.v_ref, ...), custom_call_target="tpu_custom_call" | custom-call | flops 8589934592 | bytes 12582912 | tf_op jit(solution)/shard_map/attend/pallas_call | solution.py:161
  161.2 6.8 %fusion.97 = (f32[1024]{0:T(1024)S(1)}, f32[2,1024,512]{1,2,0:T(8,128)S(1)}, f32[2,512,1024,1]{2,1,3,0:T(8,128)}) fusion(f32[2,512]{1,0:T(2,128)S(1)} %add.256, bf16[2,1024,512]{1,2,0:T(8,128)(2,1)S(1)} %bitcast.373, bf16[8,1024,128]{2,1,0:T(8,128)(2,1)} %get-tuple-element.21.o_ref, bf16[2,8,4,512,128]{4,3,2,1,0:T(8,128)(2,1)} %bitcast.410), kind=kOutput, calls=%fused_computation.171 | convolution fusion | flops 2151676928 | bytes 14688256 | tf_op jit(solution)/shard_map/ntc,sndc->std/dot_general | solution.py:257
  168.0 2.0 copy-done.4
  170.5 23.4 %fusion.4 = (bf16[8,1024,512]{2,1,0:T(8,128)(2,1)}, bf16[8,1024,512]{2,1,0:T(8,128)(2,1)}) fusion(f32[8,512]{1,0:T(8,128)S(1)} %slice.138, bf16[2,8,512,512]{3,2,1,0:T(8,128)(2,1)} %bitcast.413, f32[2,1024,512]{1,2,0:T(8,128)} %copy-done.4, f32[2,512]{1,0:T(2,128)S(1)} %add.263, f32[2,512]{1,0:T(2,128)S(1)} %mul.195, f32[1024]{0:T(1024)S(1)} %add_rsqrt_fusion.1, ...), kind=kOutput, calls=%fused_computation.5 | convolution fusion | flops 8645509120 | bytes 29392896 | tf_op jit(solution)/shard_map/std,sndf->ntf/dot_general | solution.py:257
  193.9 44.3 %all-gather.13.cloned.1.call-done = bf16[8192,512]{1,0:T(8,128)(2,1)} async-done(((bf16[512,512]{1,0:T(8,128)(2,1)}), bf16[8192,512]{1,0:T(8,128)(2,1)}) %all-gather.13.cloned.1.call-update) | async-done | bytes 8388624 | tf_op jit(solution)/shard_map/all_gather | solution.py:208
  238.2 17.1 %fusion.95 = (f32[1024]{0:T(1024)S(1)}, f32[2,1024,512]{1,2,0:T(8,128)}, f32[1024,2,512,1]{0,2,3,1:T(8,128)}) fusion(f32[2,512]{1,0:T(2,128)S(1)} %add.275, f32[2,512]{1,0:T(2,128)S(1)} %add.263, f32[2,512]{1,0:T(2,128)S(1)} %mul.195, f32[1024]{0:T(1024)S(1)} %add_rsqrt_fusion.1, f32[2,1024,512]{1,2,0:T(8,128)} %copy-done.4, ...), kind=kOutput, calls=%fused_computation.170 | convolution fusion | flops 8597273600 | bytes 29384704 | tf_op jit(solution)/shard_map/ntf,snfd->std/dot_general | solution.py:257
  255.4 2.8 multiply_reduce_fusion.4
  258.8 4.2 multiply_reduce_fusion
  263.1 1.0 subtract_multiply_fusion.1
  264.2 1.2 slice-done.1
  265.4 11.1 %fusion.21 = bf16[2,512,8,512]{3,1,2,0:T(8,128)(2,1)} fusion(bf16[8,1024,512]{2,1,0:T(8,128)(2,1)S(1)} %bitcast.419, f32[2,1024,512]{1,2,0:T(8,128)S(1)} %subtract_multiply_fusion.1), kind=kOutput, calls=%fused_computation.28 | convolution fusion | flops 8595177472 | bytes 20971520 | tf_op jit(solution)/shard_map/ntf,std->sndf/dot_general | solution.py:257
  276.5 18.1 %fusion.6 = (f32[8,512]{1,0:T(8,128)S(1)}, f32[1024,8,512,1]{2,0,1,3:T(8,128)}) fusion(bf16[8,1024,512]{2,1,0:T(8,128)(2,1)} %get-tuple-element.23, bf16[2,8,512,512]{3,2,1,0:T(8,128)(2,1)} %bitcast.416, f32[2,1024,512]{1,2,0:T(8,128)} %copy-done.8), kind=kOutput, calls=%fused_computation.11 | convolution fusion | flops 8603561984 | bytes 37765120 | tf_op jit(solution)/shard_map/std,snfd->ntf/dot_general | solution.py:257
  294.6 21.8 %multiply_reduce_fusion.1 = (f32[2,512]{1,0:T(2,128)S(1)}, f32[1024]{0:T(1024)S(1)}, f32[1024]{0:T(1024)S(1)}, f32[2,512]{1,0:T(2,128)S(1)}, f32[2,1024,512]{1,2...) fusion(f32[2,1024,512]{1,2,0:T(8,128)} %copy-done.4, f32[1024]{0:T(1024)S(1)} %add_rsqrt_fusion.1, ...), kind=kOutput, calls=%fused_computation.59 | convolution fusion | flops 8614046720 | bytes 50364416 | tf_op jit(solution)/shard_map/ntf,sndf->std/dot_general | solution.py:257
  316.5 4.9 fusion.94
  321.4 6.1 fusion.74.do_ref
  327.5 63.0 %attend_back.1 = (bf16[8,1024,128]{2,1,0:T(8,128)(2,1)}, bf16[8,1024,128]{2,1,0:T(8,128)(2,1)}, bf16[8,1024,128]{2,1,0:T(8,128)(2,1)}) custom-call(s32[1,4,4]{2,1,0:T(4,128)} %pad_add_fusion.bounds, bf16[8,1024,128]{2,1,0:T(8,128)(2,1)} %fusion.47.q_ref, bf16[8,1024,128]{2,1,0:T(8,128)(2,1)} %fusion.48.k_ref, bf16[8,1024,128]{2,1,0:T(8,128)(2,1)} %fusion.28.v_ref, ...), custom_call_target="tpu_custom_call" | custom-call | flops 21474836480 | bytes 25165824 | tf_op jit(solution)/shard_map/attend_back/pallas_call | solution.py:186
  390.6 4.1 convert_bitcast_fusion.1
  394.8 2.4 convert_bitcast_fusion.2
  397.2 2.4 convert_bitcast_fusion.3
  399.6 2.4 convert_bitcast_fusion
  402.0 3.9 pad_maximum_fusion
  405.9 7.6 %copy.141 = bf16[2,8,4,128,512]{4,3,2,1,0:T(8,128)(2,1)} copy(bf16[2,8,4,128,512]{4,3,0,1,2:T(8,128)(2,1)} %pad_maximum_fusion) | data formatting | bytes 16777216 | tf_op jit(solution)/shard_map/stack | solution.py:390
  413.5 0.6 copy-done.24
  414.1 17.4 %convolution_convert_fusion = bf16[2,512,8,512]{3,1,2,0:T(8,128)(2,1)} fusion(f32[2,1024,512]{1,2,0:T(8,128)} %copy-done.4, f32[2,512]{1,0:T(2,128)S(1)} %copy-done.24, f32[2,512]{1,0:T(2,128)S(1)} %mul.195, f32[1024]{0:T(1024)S(1)} %add_rsqrt_fusion.1, f32[1024]{0:T(1024)S(1)} %broadcast_multiply_fusion.5, bf16[8,1024,512]{2,1,0:T(8,128)(2,1)} %get-tuple-element.23, ...), kind=kOutput, calls=%fused_computation.29 | convolution fusion | flops 8611954688 | bytes 37765120 | tf_op jit(solution)/shard_map/ntf,std->sndf/dot_general | solution.py:257
  432.3 1.9 convert_reduce_fusion.1
  434.2 1.9 convert_reduce_fusion
  436.1 1.6 collective-permute-start.1
  437.7 2.6 collective-permute-done.1
  440.3 27.8 %collective-permute-start.2 = (f32[96,128]{1,0:T(8,128)S(1)}, f32[96,128]{1,0:T(8,128)S(1)}, u32[]{:S(2)}, u32[]{:S(2)}) collective-permute-start(f32[96,128]{1,0:T(8,128)S(1)} %bitcast_add_fusion.8), channel_id=1, source_target_pairs={{0,8},{8,0},{1,9},{9,1},{2,10},{10,2},{3,11},{11,3},{4,12},{12,4},... | collective-permute-start | bytes 147464 | tf_op jit(solution)/shard_map/ppermute | solution.py:251
  468.0 2.4 collective-permute-done.2
  470.6 1.2 collective-permute-done.3
  471.8 2.2 collective-permute-start.4
  474.0 20.2 %bitcast_add_fusion.1 = f32[1024,2,512]{0,2,1:T(8,128)} fusion(f32[1024,2,512,1]{0,2,3,1:T(8,128)} %get-tuple-element.122, f32[1024,2,512]{0,2,1:T(8,128)} %bitcast.367, f32[1024,2,512,1]{0,2,3,1:T(8,128)} %get-tuple-element.121, bf16[1,8,1024,128]{3,2,1,0:T(8,128)(2,1)} %bitcast.382, bf16[1,8,1024,128]{3,2,1,0:T(8,128)(2,1)} %bitcast.417, ...), kind=kOutput, calls=%fused_computation.38 | convolution fusion | flops 6485442560 | bytes 35704832 | tf_op jit(solution)/shard_map/jntc,snjdc->std/dot_general | solution.py:257
  494.6 5.6 add_convert_fusion
  500.3 5.6 copy.143
  505.8 2.5 copy.142
  508.4 2.1 collective-permute-start.7
  510.5 0.7 dynamic_slice.12
  511.1 33.2 %reduce-scatter.4.cloned.1.call-done = bf16[512,512]{1,0:T(8,128)(2,1)} async-done(((bf16[8192,512]{1,0:T(8,128)(2,1)}), bf16[512,512]{1,0:T(8,128)(2,1)}) %reduce-scatter.4.cloned.1.call-update) | async-done | bytes 524304 | tf_op jit(solution)/shard_map/reduce_scatter | solution.py:231
  544.3 1.5 collective-permute-start
  545.8 0.6 slice_bitcast_fusion.10
  546.4 0.6 fusion.85
  547.0 104.3 %reduce-scatter.6.cloned.1.call-done = bf16[512,512]{1,0:T(8,128)(2,1)} async-done(((bf16[8192,512]{1,0:T(8,128)(2,1)}), bf16[512,512]{1,0:T(8,128)(2,1)}) %reduce-scatter.6.cloned.1.call-update) | async-done | bytes 524304 | tf_op jit(solution)/shard_map/reduce_scatter | solution.py:231
  651.3 1.5 collective-permute-start.6
  652.8 1.2 add_bitcast_fusion
  654.0 1.2 convert_add_fusion.1
  655.2 1.3 copy.145
  656.6 1.1 copy.144
  657.8 0.7 slice_bitcast_fusion.8
  658.5 6.4 collective-permute-done.6
  664.9 2.2 convert_add_fusion
  (154 shorter events, 3.9 us)
Async XLA Ops:
  7.2 4.6 copy-start
  7.2 7.6 %copy-start.38 = (f32[2,128]{1,0:T(2,128)S(1)}, f32[2,128]{1,0:T(2,128)}, u32[]{:S(2)}) copy-start(f32[2,128]{1,0:T(2,128)} %param.18) | copy-start | bytes 3076
  7.2 7.7 %copy-start.37 = (f32[512]{0:T(512)S(1)}, f32[512]{0:T(512)}, u32[]{:S(2)}) copy-start(f32[512]{0:T(512)} %param.24) | copy-start | bytes 6148
  7.2 23.6 %copy-start.31 = (f32[1024]{0:T(1024)S(1)}, f32[1024]{0:T(1024)}, u32[]{:S(2)}) copy-start(f32[1024]{0:T(1024)} %param.20) | copy-start | bytes 12292
  7.2 23.6 %copy-start.32 = (f32[1024]{0:T(1024)S(1)}, f32[1024]{0:T(1024)}, u32[]{:S(2)}) copy-start(f32[1024]{0:T(1024)} %param.21) | copy-start | bytes 12292
  7.2 23.6 %copy-start.33 = (f32[1024]{0:T(1024)S(1)}, f32[1024]{0:T(1024)}, u32[]{:S(2)}) copy-start(f32[1024]{0:T(1024)} %param.22) | copy-start | bytes 12292
  7.2 23.6 %copy-start.34 = (f32[1024]{0:T(1024)S(1)}, f32[1024]{0:T(1024)}, u32[]{:S(2)}) copy-start(f32[1024]{0:T(1024)} %param.26) | copy-start | bytes 12292
  7.3 80.7 %all-gather.9.cloned.1.call-start = ((), (), s32[]{:S(2)}) async-start(), calls=%async_computation.6 | async-start | bytes 8912896 | tf_op jit(solution)/shard_map/all_gather | solution.py:208
  10.2 160.3 %all-gather.11.cloned.1.call-start = ((), (), s32[]{:S(2)}) async-start(), calls=%async_computation.7 | async-start | bytes 8912896 | tf_op jit(solution)/shard_map/all_gather | solution.py:208
  10.9 227.3 %all-gather.13.cloned.1.call-start = ((), (), s32[]{:S(2)}) async-start(), calls=%async_computation.8 | async-start | bytes 8912896 | tf_op jit(solution)/shard_map/all_gather | solution.py:208
  11.7 496.7 %reduce-scatter.8.cloned.1.call-start = ((), (), s32[]{:S(2)}) async-start(), calls=%async_computation.5 | async-start | bytes 8912896 | tf_op jit(solution)/shard_map/reduce_scatter | solution.py:231
  14.8 146.3 %copy-start.5 = (bf16[1024,1024]{0,1:T(8,128)(2,1)}, bf16[1024,1024]{0,1:T(8,128)(2,1)S(1)}, u32[]{:S(2)}) copy-start(bf16[1024,1024]{0,1:T(8,128)(2,1)S(1)} %copy.116) | copy-start | bytes 6291460
  14.9 20.2 %copy-start.35 = (f32[1024]{0:T(1024)S(1)}, f32[1024]{0:T(1024)}, u32[]{:S(2)}) copy-start(f32[1024]{0:T(1024)} %param.27) | copy-start | bytes 12292
  30.8 130.4 %copy-start.21 = (f32[2,512]{1,0:T(2,128)}, f32[2,512]{1,0:T(2,128)S(1)}, u32[]{:S(2)}) copy-start(f32[2,512]{1,0:T(2,128)S(1)} %add.256) | copy-start | bytes 12292
  30.9 207.4 %copy-start.23 = (f32[2,512]{1,0:T(2,128)}, f32[2,512]{1,0:T(2,128)S(1)}, u32[]{:S(2)}) copy-start(f32[2,512]{1,0:T(2,128)S(1)} %add.263) | copy-start | bytes 12292
  30.9 207.3 %copy-start.25 = (f32[2,512]{1,0:T(2,128)}, f32[2,512]{1,0:T(2,128)S(1)}, u32[]{:S(2)}) copy-start(f32[2,512]{1,0:T(2,128)S(1)} %add.275) | copy-start | bytes 12292
  35.1 228.0 %copy-start.15 = (f32[2,512]{1,0:T(2,128)}, f32[2,512]{1,0:T(2,128)S(1)}, u32[]{:S(2)}) copy-start(f32[2,512]{1,0:T(2,128)S(1)} %mul.216) | copy-start | bytes 12292
  168.0 2.0 copy-start.4
  255.3 3.5 copy-start.2
  255.4 7.7 %copy-start.13 = (f32[1024]{0:T(1024)}, f32[1024]{0:T(1024)S(1)}, u32[]{:S(2)}) copy-start(f32[1024]{0:T(1024)S(1)} %broadcast_multiply_fusion.4) | copy-start | bytes 12292
  258.2 4.9 copy-start.17
  258.8 4.3 copy-start.3
  258.8 5.4 slice-start
  263.0 2.3 slice-start.1
  263.0 1.1 copy-start.27
  263.1 1.1 copy-start.29
  265.4 11.1 %copy-start.8 = (f32[2,1024,512]{1,2,0:T(8,128)}, f32[2,1024,512]{1,2,0:T(8,128)S(1)}, u32[]{:S(2)}) copy-start(f32[2,1024,512]{1,2,0:T(8,128)S(1)} %subtract_multiply_fusion.1) | copy-start | bytes 12582916
  276.5 267.8 %reduce-scatter.4.cloned.1.call-start = ((), (), s32[]{:S(2)}) async-start(), calls=%async_computation.3 | async-start | bytes 8912896 | tf_op jit(solution)/shard_map/reduce_scatter | solution.py:231
  321.4 6.1 copy-start.10
  327.5 63.1 %copy-start.6 = (bf16[1024,1024]{0,1:T(8,128)(2,1)S(1)}, bf16[1024,1024]{0,1:T(8,128)(2,1)}, u32[]{:S(2)}) copy-start(bf16[1024,1024]{0,1:T(8,128)(2,1)} %copy-done.5) | copy-start | bytes 6291460
  390.6 4.1 copy-start.39
  394.7 2.4 copy-start.9
  397.2 2.4 copy-start.11
  397.2 2.4 copy-start.40
  413.5 0.7 copy-start.24
  413.5 237.8 %reduce-scatter.6.cloned.1.call-start = ((), (), s32[]{:S(2)}) async-start(), calls=%async_computation.4 | async-start | bytes 8912896 | tf_op jit(solution)/shard_map/reduce_scatter | solution.py:231
  431.6 0.7 copy-start.20
  431.6 0.7 copy-start.19
  431.6 38.9 %copy-start.36 = (f32[1024]{0:T(1024)S(1)}, f32[1024]{0:T(1024)}, u32[]{:S(2)}) copy-start(f32[1024]{0:T(1024)} %param.28) | copy-start | bytes 12292
  431.6 42.4 %copy-start.14 = (f32[1024]{0:T(1024)S(1)}, f32[1024]{0:T(1024)}, u32[]{:S(2)}) copy-start(f32[1024]{0:T(1024)} %copy-done.13) | copy-start | bytes 12292
  431.6 42.3 %copy-start.16 = (f32[2,512]{1,0:T(2,128)S(1)}, f32[2,512]{1,0:T(2,128)}, u32[]{:S(2)}) copy-start(f32[2,512]{1,0:T(2,128)} %copy-done.15) | copy-start | bytes 12292
  431.6 42.3 %copy-start.18 = (f32[1024]{0:T(1024)S(1)}, f32[1024]{0:T(1024)}, u32[]{:S(2)}) copy-start(f32[1024]{0:T(1024)} %copy-done.17) | copy-start | bytes 12292
  431.7 42.3 %copy-start.22 = (f32[2,512]{1,0:T(2,128)S(1)}, f32[2,512]{1,0:T(2,128)}, u32[]{:S(2)}) copy-start(f32[2,512]{1,0:T(2,128)} %copy-done.21) | copy-start | bytes 12292
  431.7 42.3 %copy-start.26 = (f32[2,512]{1,0:T(2,128)S(1)}, f32[2,512]{1,0:T(2,128)}, u32[]{:S(2)}) copy-start(f32[2,512]{1,0:T(2,128)} %copy-done.25) | copy-start | bytes 12292
  431.7 42.3 %copy-start.28 = (f32[1024]{0:T(1024)S(1)}, f32[1024]{0:T(1024)}, u32[]{:S(2)}) copy-start(f32[1024]{0:T(1024)} %copy-done.27) | copy-start | bytes 12292
  431.7 42.3 %copy-start.30 = (f32[1024]{0:T(1024)S(1)}, f32[1024]{0:T(1024)}, u32[]{:S(2)}) copy-start(f32[1024]{0:T(1024)} %copy-done.29) | copy-start | bytes 12292
  436.1 4.2 collective-permute-start.1
  440.3 30.2 %collective-permute-start.2 = (f32[96,128]{1,0:T(8,128)S(1)}, f32[96,128]{1,0:T(8,128)S(1)}, u32[]{:S(2)}, u32[]{:S(2)}) collective-permute-start(f32[96,128]{1,0:T(8,128)S(1)} %bitcast_add_fusion.8), channel_id=1, source_target_pairs={{0,8},{8,0},{1,9},{9,1},{2,10},{10,2},{3,11},{11,3},{4,12},{12,4},... | collective-permute-start | bytes 147464 | tf_op jit(solution)/shard_map/ppermute | solution.py:251
  470.5 1.3 collective-permute-start.3
  471.8 22.4 %collective-permute-start.4 = (f32[96,128]{1,0:T(8,128)S(1)}, f32[96,128]{1,0:T(8,128)S(1)}, u32[]{:S(2)}, u32[]{:S(2)}) collective-permute-start(f32[96,128]{1,0:T(8,128)S(1)} %add.291), channel_id=1, source_target_pairs={{0,2},{1,3},{2,0},{3,1},{4,6},{5,7},{6,4},{7,5},{8,10},{9,11},{10,... | collective-permute-start | bytes 147464 | tf_op jit(solution)/shard_map/ppermute | solution.py:251
  494.2 14.2 %collective-permute-start.5 = (f32[96,128]{1,0:T(8,128)S(1)}, f32[96,128]{1,0:T(8,128)S(1)}, u32[]{:S(2)}, u32[]{:S(2)}) collective-permute-start(f32[96,128]{1,0:T(8,128)S(1)} %add.292), channel_id=1, source_target_pairs={{0,4},{1,5},{2,6},{3,7},{4,0},{5,1},{6,2},{7,3},{8,12},{9,13},{10,... | collective-permute-start | bytes 147464 | tf_op jit(solution)/shard_map/ppermute | solution.py:251
  500.3 5.6 copy-start.7
  508.4 144.4 %collective-permute-start.7 = (bf16[512,512]{1,0:T(8,128)(2,1)}, bf16[512,512]{1,0:T(8,128)(2,1)S(1)}, u32[]{:S(2)}, u32[]{:S(2)}) collective-permute-start(bf16[512,512]{1,0:T(8,128)(2,1)} %reduce-scatter.8.cloned.1.call-done), channel_id=1, source_target_pairs={{0,16},{16,0},{1,17},{17,1},{2,18},{18,2},{3,19},{19,3},{4,20},{20... | collective-permute-start | bytes 1572872 | tf_op jit(solution)/shard_map/ppermute | solution.py:241
  544.3 109.7 %collective-permute-start = (bf16[4,128,512]{2,1,0:T(8,128)(2,1)}, bf16[4,128,512]{2,1,0:T(8,128)(2,1)S(1)}, u32[]{:S(2)}, u32[]{:S(2)}) collective-permute-start(bf16[4,128,512]{2,1,0:T(8,128)(2,1)} %bitcast.383), channel_id=1, source_target_pairs={{0,16},{16,0},{1,17},{17,1},{2,18},{18,2},{3,19},{19,3},{4,20},{20... | collective-permute-start | bytes 1572872 | tf_op jit(solution)/shard_map/ppermute | solution.py:241
  651.3 13.6 %collective-permute-start.6 = (bf16[512,512]{1,0:T(8,128)(2,1)}, bf16[512,512]{1,0:T(8,128)(2,1)}, u32[]{:S(2)}, u32[]{:S(2)}) collective-permute-start(bf16[512,512]{1,0:T(8,128)(2,1)} %reduce-scatter.6.cloned.1.call-done), channel_id=1, source_target_pairs={{0,16},{16,0},{1,17},{17,1},{2,18},{18,2},{3,19},{19,3},{4,20},{20... | collective-permute-start | bytes 1572872 | tf_op jit(solution)/shard_map/ppermute | solution.py:241
  654.0 10.9 %copy-start.12 = (bf16[512,512]{1,0:T(8,128)(2,1)S(1)}, bf16[512,512]{1,0:T(8,128)(2,1)}, u32[]{:S(2)}) copy-start(bf16[512,512]{1,0:T(8,128)(2,1)} %reduce-scatter.6.cloned.1.call-done) | copy-start | bytes 1572868
  654.0 13.1 %copy-start.1 = (s32[8,1024]{1,0:T(8,128)S(1)}, s32[8,1024]{1,0:T(8,128)}, u32[]{:S(2)}) copy-start(s32[8,1024]{1,0:T(8,128)} %param.16) | copy-start | bytes 98308
Sparse Core Ops, SparseCore 0:
  10.8 77.0 all-gather.8
  90.2 72.8 all-gather.10
  165.3 72.8 all-gather.12
  276.6 102.0 reduce-scatter.7
  413.6 130.6 reduce-scatter.3
  548.2 103.0 reduce-scatter.5

commit v3 on v2

--- a/solution.py
+++ b/solution.py
@@ -177,28 +177,37 @@
     )(bounds, q, k, v, q_mark, k_mark)
 
 
-def attend_back(q, k, v, q_mark, k_mark, bounds, lse, o, do, kv_type):
-    pairs, seqs = q.shape[0], q_mark.shape[0]
+def attend_back(q, k, v, q_mark, k_mark, bounds, lse, o, do, kv_type, first, count):
+    seqs = q_mark.shape[0]
     rows = q.shape[1] // seqs
-    q_spec, qm_spec = specs(rows)
-    k_spec, km_spec = specs(LEN)
-    lse_spec = pl.BlockSpec((None, None, 2, rows), lambda s, p, b: (s, p, 0, 0))
+
+    def own(length):
+        return pl.BlockSpec((None, length, PAIR), lambda s, p, b: (p + first, s, 0))
+
+    def result(length):
+        return pl.BlockSpec((None, length, PAIR), lambda s, p, b: (p, s, 0))
+
+    _, qm_spec = specs(rows)
+    _, km_spec = specs(LEN)
+    lse_spec = pl.BlockSpec((None, None, 2, rows), lambda s, p, b: (s, p + first, 0, 0))
     return pl.pallas_call(
         attend_back_kernel,
         grid_spec=pltpu.PrefetchScalarGridSpec(
             num_scalar_prefetch=1,
-            grid=(seqs, pairs),
-            in_specs=[q_spec, k_spec, k_spec, qm_spec, km_spec, lse_spec, q_spec, q_spec],
-            out_specs=[q_spec, k_spec, k_spec],
+            grid=(seqs, count),
+            in_specs=[own(rows), own(LEN), own(LEN), qm_spec, km_spec, lse_spec, own(rows), own(rows)],
+            out_specs=[result(rows), result(LEN), result(LEN)],
             scratch_shapes=[pltpu.VMEM((rows, PAIR), jnp.float32), pltpu.VMEM((2, rows), jnp.float32)],
         ),
         out_shape=[
-            jax.ShapeDtypeStruct(q.shape, kv_type),
-            jax.ShapeDtypeStruct(k.shape, kv_type),
-            jax.ShapeDtypeStruct(k.shape, kv_type),
+            jax.ShapeDtypeStruct((count,) + q.shape[1:], kv_type),
+            jax.ShapeDtypeStruct((count,) + k.shape[1:], kv_type),
+            jax.ShapeDtypeStruct((count,) + k.shape[1:], kv_type),
         ],
         cost_estimate=pl.CostEstimate(
-            flops=20 * q.size * LEN, bytes_accessed=24 * k.size, transcendentals=2 * rows * LEN * pairs
+            flops=20 * count * rows * seqs * PAIR * LEN,
+            bytes_accessed=24 * count * k.shape[1] * PAIR,
+            transcendentals=2 * rows * LEN * count * seqs,
         ),
         name="attend_back",
     )(bounds, q, k, v, q_mark, k_mark, lse, o, do)
@@ -231,6 +240,31 @@
     owned = lax.psum_scatter(flat, OWNERS, scatter_dimension=0, tiled=True)
     owned = with_layout_constraint(owned, Layout(major_to_minor=(0, 1)))
     return owned.reshape(block_shape)
+
+
+def fold_replicas(blocks):
+    count, me = lax.axis_size("replica"), lax.axis_index("replica")
+    owners, rows, cols = blocks.shape
+    parts = blocks.reshape(owners, count, rows // count, cols)
+    total = lax.dynamic_index_in_dim(parts, me, 1, keepdims=False).astype(jnp.float32)
+    for step in range(1, count):
+        ring = [(i, (i + step) % count) for i in range(count)]
+        sent = lax.dynamic_index_in_dim(parts, (me + step) % count, 1, keepdims=False)
+        total = total + lax.ppermute(sent, "replica", ring).astype(jnp.float32)
+    return total.astype(jnp.bfloat16)
+
+
+def unfold_replicas(owned):
+    count, me = lax.axis_size("replica"), lax.axis_index("replica")
+    arrived = [owned]
+    for step in range(1, count):
+        ring = [(i, (i + step) % count) for i in range(count)]
+        arrived.append(lax.ppermute(owned, "replica", ring))
+    arrived = jnp.stack(arrived).astype(jnp.float32)
+    parts = [
+        lax.dynamic_index_in_dim(arrived, (me - k) % count, 0, keepdims=False) for k in range(count)
+    ]
+    return jnp.concatenate(parts, axis=0)
 
 
 def over_replicas(owned):
@@ -371,7 +405,9 @@
     up_bias_part = jnp.sum(pre_grad, axis=1)
     pre_low = pre_grad.astype(jnp.bfloat16)
     up_grad = dot("ntf,std->sndf", pre_low, hidden_low).astype(jnp.bfloat16)
-    up_owned = scatter_blocks(up_grad, up_weight.shape)
+    owners = shards * tensors
+    up_folded = fold_replicas(up_grad.reshape((owners,) + up_weight.shape))
+    up_owned = scatter_blocks(up_folded, up_folded.shape[1:])
     back_middle = dot("ntf,sndf->std", pre_low, w_up)
     resid_one_grad, gain_one_grad, shift_one_grad = norm_back(
         resid_two_grad + back_middle, normed_one, spread_one, vec(norm1_gain)
@@ -381,22 +417,51 @@
     out_grad = dot("ntc,std->sncd", mixed, attn_grad).astype(jnp.bfloat16)
     mixed_grad = dot("std,sndc->ntc", attn_grad, w_out).astype(jnp.bfloat16)
     grad_type = jnp.bfloat16 if sharers == 1 else jnp.float32
-    query_grad, key_grad, value_grad = attend_back(
-        queries, key_rows, value_rows, q_mark, k_mark, bounds, log_total, mixed, mixed_grad, grad_type
-    )
+    half = pairs // 2
+    grads = []
+    for first, count in ((0, half), (half, pairs - half)):
+        grads.append(
+            attend_back(
+                queries,
+                key_rows,
+                value_rows,
+                q_mark,
+                k_mark,
+                bounds,
+                log_total,
+                mixed,
+                mixed_grad,
+                grad_type,
+                first,
+                count,
+            )
+        )
+    query_grad, key_grad, value_grad = [jnp.concatenate(both) for both in zip(*grads)]
     key_grad, value_grad = own_rows(key_grad), own_rows(value_grad)
     proj_low = jnp.stack([query_grad, key_grad, value_grad]).astype(jnp.bfloat16)
-    qkv_grad = [dot("ntc,std->sncd", proj_low[j], tokens).astype(jnp.bfloat16) for j in range(3)]
-    attn_weight_grad = jnp.stack(qkv_grad + [out_grad], axis=2)
-    attn_owned = scatter_blocks(
-        unpair_blocks(attn_weight_grad, tensors), (4,) + out_weight.shape
-    )
+
+    def weight_grad(j):
+        return dot("ntc,std->sncd", proj_low[j], tokens).astype(jnp.bfloat16)
+
+    def by_owner(grads):
+        blocks = unpair_blocks(jnp.stack(grads, axis=2), tensors)
+        return blocks.reshape(owners, -1, width // shards)
+
+    query_key_grad = by_owner([weight_grad(0), weight_grad(1)])
+    query_key_folded = fold_replicas(query_key_grad)
+    value_out_grad = by_owner([weight_grad(2), out_grad])
+    value_out_owned = scatter_blocks(value_out_grad, (2,) + out_weight.shape)
+    down_owned = over_replicas(down_owned).T
+    up_owned = unfold_replicas(up_owned)
+    query_key_folded, down_owned, up_owned = lax.optimization_barrier(
+        (query_key_folded, down_owned, up_owned)
+    )
+    query_key_owned = scatter_blocks(query_key_folded, query_key_folded.shape[1:])
     back_input = dot("jntc,snjdc->std", proj_low, w_qkv)
     input_grad = resid_one_grad + back_input
-    down_owned = over_replicas(down_owned).T
-    up_owned = over_replicas(up_owned)
-    attn_owned = over_replicas(attn_owned)
-    qkv_owned, out_owned = attn_owned[:3].transpose(0, 2, 1), attn_owned[3]
+    query_key_owned = unfold_replicas(query_key_owned).reshape((2,) + out_weight.shape)
+    value_owned, out_owned = over_replicas(value_out_owned)
+    qkv_owned = jnp.concatenate([query_key_owned, value_owned[None]]).transpose(0, 2, 1)
     parts = (
         jnp.sum(query_grad.astype(jnp.float32), axis=1),
         jnp.sum(value_grad.astype(jnp.float32), axis=1),

time: 684 us -> 748 us (1.094)
  starting transfers between devices: 37.3 us -> 60.6 us
  waiting for transfers between devices: 247 us -> 262 us
  local copies, waits for them, and re-layouts: 35.3 us -> 47.8 us
    reduce_scatter x3 -> x4, waiting for transfers between devices: 137 us -> 31.9 us  [scatter_blocks(): owned = lax.psum_scatter(flat, OWNERS, scatter_dimension=0, tiled=True)]
    ppermute x0 -> x4, waiting for transfers between devices: none -> 96.5 us  [the longest x2 91.6 us: fold_replicas(): total = total + lax.ppermute(sent, 'replica', ring).astype(jnp.float32)]
    ppermute x5, waiting for transfers between devices: 6.19 us -> 28.1 us  [sum_over(): lax.ppermute(values, axis, [(i, i ^ step) for i in range(count)])]
    ppermute x5, starting transfers between devices: 32.1 us -> 51.9 us  [sum_over(): lax.ppermute(values, axis, [(i, i ^ step) for i in range(count)])]
    convert_element_type x0 -> x4, other arithmetic: none -> 11.9 us  [the longest x2 10.9 us: fold_replicas(): return total.astype(jnp.bfloat16)]
    unnamed x109 -> x104, local copies, waits for them, and re-layouts: 19.6 us -> 23.6 us
    pallas_call x1 -> x2, Pallas kernels: 63 us -> 66.6 us  [attend_back(): pl.pallas_call(attend_back_kernel, grid_spec=pltpu.PrefetchScalarGridSpec...]
  transfers between devices with their start and end apart: 14 -> 18, of which waited for: 8 -> 11; matrix products, arithmetic and copies ran while one was open for 28% -> 24% of each run, Pallas kernels for 18% -> 17%
where the time goes in v3:
time: 748 us; the launch traced here: 738 us
  waiting for transfers between devices  262 us (35%)
  matrix products  166 us (22%)
  Pallas kernels  125 us (17%)
  starting transfers between devices  60.6 us (8%)
  local copies, waits for them, and re-layouts  47.8 us (6%)
  other arithmetic  45.1 us (6%)
  blocking collectives  16 us (2%)
  between operations  15.2 us (2%)
    dot_general x14, matrix products, dot(): return jnp.einsum(spec, left, right, preferred_element_type=jnp.float32)  166 us
    ppermute x2, waiting for transfers between devices, fold_replicas(): total = total + lax.ppermute(sent, 'replica', ring).astype(jnp.float32)  91.6 us
    all_gather x3, waiting for transfers between devices, gather_blocks(): blocks = lax.all_gather(weight, OWNERS, axis=0, tiled=False)  90.2 us
    pallas_call x2, Pallas kernels, attend_back(): pl.pallas_call(attend_back_kernel, grid_spec=pltpu.PrefetchScalarGridSpec...  66.6 us
    pallas_call x1, Pallas kernels, attend(): pl.pallas_call(attend_kernel, grid_spec=pltpu.PrefetchScalarGridSpec(num_...  58.9 us
    ppermute x5, starting transfers between devices, sum_over(): lax.ppermute(values, axis, [(i, i ^ step) for i in range(count)])  51.9 us
    reduce_scatter x4, waiting for transfers between devices, scatter_blocks(): owned = lax.psum_scatter(flat, OWNERS, scatter_dimension=0, tiled=True)  31.9 us
    ppermute x5, waiting for transfers between devices, sum_over(): lax.ppermute(values, axis, [(i, i ^ step) for i in range(count)])  28.1 us
  transfers between devices with their start and end apart: 18, of which 11 were waited for; matrix products, arithmetic and copies ran while one was open for 24% of the time, Pallas kernels for 17%

profile of v3, /device:TPU:0, one launch (start us, length us, event | category | flops | bytes accessed | tf_op | source)
XLA Modules:
  0.0 738.0 jit_solution(16153101600524947747)
XLA Ops:
  7.2 1.0 copy.124
  8.3 1.8 pad_maximum_fusion.2
  16.9 16.0 %all-gather.4 = f32[8,1,768]{2,1,0:T(1,128)S(1)} all-gather(f32[1,1,768]{2,1,0:T(1,128)S(1)} %reshape.806), channel_id=3, replica_groups=mesh['replica'=2,'shard'=2,'tensor'=8] {'tensor'}, dimensions={0}, use_global_device_ids=true | all-gather | bytes 27648 | tf_op jit(solution)/shard_map/all_gather | solution.py:343
  32.9 2.9 copy.123
  35.7 4.8 copy.132
  41.4 1.0 fusion.89
  42.4 45.6 %all-gather.9.cloned.1.call-done = bf16[64,512,128]{2,1,0:T(8,128)(2,1)} async-done(((bf16[4,512,128]{2,1,0:T(8,128)(2,1)}), bf16[64,512,128]{2,1,0:T(8,128)(2,1)}) %all-gather.9.cloned.1.call-update) | async-done | bytes 8388624 | tf_op jit(solution)/shard_map/all_gather | solution.py:217
  88.0 9.2 %fusion.25 = f32[3,8,1024,128]{3,2,1,0:T(8,128)S(1)} fusion(bf16[2,1024,512,1,1]{1,2,0,3,4:T(8,128)(2,1)S(1)} %bitcast.405, bf16[2,8,4,512,128]{4,3,2,1,0:T(8,128)(2,1)} %bitcast.449), kind=kOutput, calls=%fused_computation.35 | convolution fusion | flops 6442450944 | bytes 20971520 | tf_op jit(solution)/shard_map/std,snjdc->jntc/dot_general | solution.py:291
  97.2 1.7 fusion.50.k_ref
  98.8 1.7 fusion.29.v_ref
  100.6 1.7 fusion.49.q_ref
  102.3 58.9 %attend.1 = (bf16[8,1024,128]{2,1,0:T(8,128)(2,1)}, f32[1,8,2,1024]{3,2,1,0:T(2,128)}) custom-call(s32[1,4,4]{2,1,0:T(4,128)} %pad_add_fusion.bounds, bf16[8,1024,128]{2,1,0:T(8,128)(2,1)} %fusion.49.q_ref, bf16[8,1024,128]{2,1,0:T(8,128)(2,1)} %fusion.50.k_ref, bf16[8,1024,128]{2,1,0:T(8,128)(2,1)} %fusion.29.v_ref, ...), custom_call_target="tpu_custom_call" | custom-call | flops 8589934592 | bytes 12582912 | tf_op jit(solution)/shard_map/attend/pallas_call | solution.py:161
  161.2 6.8 fusion.103
  167.9 2.0 copy-done.5
  170.4 23.2 %fusion.4 = (bf16[8,1024,512]{2,1,0:T(8,128)(2,1)}, bf16[8,1024,512]{2,1,0:T(8,128)(2,1)}) fusion(f32[8,512]{1,0:T(8,128)S(1)} %slice.130, bf16[2,8,512,512]{3,2,1,0:T(8,128)(2,1)} %bitcast.453, f32[2,1024,512]{1,2,0:T(8,128)} %copy-done.5, f32[2,512]{1,0:T(2,128)S(1)} %add.305, f32[2,512]{1,0:T(2,128)S(1)} %mul.195, f32[1024]{0:T(1024)S(1)} %add_rsqrt_fusion.1, ...), kind=kOutput, calls=%fused_computation.5 | convolution fusion | flops 8645509120 | bytes 29392896 | tf_op jit(solution)/shard_map/std,sndf->ntf/dot_general | solution.py:291
  193.6 44.6 %all-gather.13.cloned.1.call-done = bf16[8192,512]{1,0:T(8,128)(2,1)} async-done(((bf16[512,512]{1,0:T(8,128)(2,1)}), bf16[8192,512]{1,0:T(8,128)(2,1)}) %all-gather.13.cloned.1.call-update) | async-done | bytes 8388624 | tf_op jit(solution)/shard_map/all_gather | solution.py:217
  238.2 17.2 %fusion.101 = (f32[1024]{0:T(1024)S(1)}, f32[2,1024,512]{1,2,0:T(8,128)}, f32[1024,2,512,1]{0,2,3,1:T(8,128)}) fusion(f32[2,512]{1,0:T(2,128)S(1)} %add.317, f32[2,512]{1,0:T(2,128)S(1)} %add.305, f32[2,512]{1,0:T(2,128)S(1)} %mul.195, f32[1024]{0:T(1024)S(1)} %add_rsqrt_fusion.1, f32[2,1024,512]{1,2,0:T(8,128)} %copy-done.5, ...), kind=kOutput, calls=%fused_computation.196 | convolution fusion | flops 8597273600 | bytes 29384704 | tf_op jit(solution)/shard_map/ntf,snfd->std/dot_general | solution.py:291
  255.5 2.8 multiply_reduce_fusion.4
  258.9 4.2 multiply_reduce_fusion
  263.2 1.0 subtract_multiply_fusion.1
  264.2 18.5 %fusion.6 = (f32[8,512]{1,0:T(8,128)S(1)}, f32[1024,8,512,1]{2,0,1,3:T(8,128)}) fusion(bf16[8,1024,512]{2,1,0:T(8,128)(2,1)} %get-tuple-element.29, bf16[2,8,512,512]{3,2,1,0:T(8,128)(2,1)} %bitcast.456, f32[2,1024,512]{1,2,0:T(8,128)S(1)} %subtract_multiply_fusion.1), kind=kOutput, calls=%fused_computation.11 | convolution fusion | flops 8603561984 | bytes 37765120 | tf_op jit(solution)/shard_map/std,snfd->ntf/dot_general | solution.py:291
  282.8 17.3 %convolution_convert_fusion = bf16[2,512,8,512]{3,1,2,0:T(8,128)(2,1)} fusion(f32[2,1024,512]{1,2,0:T(8,128)} %copy-done.5, f32[2,512]{1,0:T(2,128)S(1)} %add.305, f32[2,512]{1,0:T(2,128)S(1)} %mul.195, f32[1024]{0:T(1024)S(1)} %add_rsqrt_fusion.1, f32[1024]{0:T(1024)S(1)} %broadcast_multiply_fusion.5, bf16[8,1024,512]{2,1,0:T(8,128)(2,1)} %get-tuple-element.29, ...), kind=kOutput, calls=%fused_computation.30 | convolution fusion | flops 8611954688 | bytes 37765120 | tf_op jit(solution)/shard_map/ntf,std->sndf/dot_general | solution.py:291
  300.1 4.5 dynamic-slice_bitcast_fusion
  304.6 1.4 collective-permute-start.2
  306.1 91.6 %collective-permute-done.2 = bf16[16,256,512]{2,1,0:T(8,128)(2,1)} collective-permute-done((bf16[16,256,512]{2,1,0:T(8,128)(2,1)}, bf16[16,256,512]{2,1,0:T(8,128)(2,1)}, u32[]{:S(2)}, u32[]{:S(2)}) %collective-permute-start.2) | collective-permute-done | bytes 4194336 | tf_op jit(solution)/shard_map/ppermute | solution.py:253
  397.7 6.8 fusion.9
  404.6 14.5 %fusion.22 = bf16[2,512,8,512]{3,1,2,0:T(8,128)(2,1)} fusion(bf16[8,1024,512]{2,1,0:T(8,128)(2,1)} %get-tuple-element.28, f32[2,1024,512]{1,2,0:T(8,128)} %copy-done.12), kind=kOutput, calls=%fused_computation.29 | convolution fusion | flops 8595177472 | bytes 20971520 | tf_op jit(solution)/shard_map/ntf,std->sndf/dot_general | solution.py:291
  419.2 21.2 %multiply_reduce_fusion.1 = (f32[2,512]{1,0:T(2,128)S(1)}, f32[1024]{0:T(1024)S(1)}, f32[1024]{0:T(1024)S(1)}, f32[2,512]{1,0:T(2,128)S(1)}, f32[2,1024,512]{1,2...) fusion(f32[2,1024,512]{1,2,0:T(8,128)} %copy-done.5, f32[1024]{0:T(1024)S(1)} %add_rsqrt_fusion.1, ...), kind=kOutput, calls=%fused_computation.67 | convolution fusion | flops 8614046720 | bytes 50364416 | tf_op jit(solution)/shard_map/ntf,sndf->std/dot_general | solution.py:291
  440.4 4.9 fusion.100
  445.4 6.1 fusion.80.do_ref
  451.5 33.0 %attend_back.2 = (bf16[4,1024,128]{2,1,0:T(8,128)(2,1)}, bf16[4,1024,128]{2,1,0:T(8,128)(2,1)}, bf16[4,1024,128]{2,1,0:T(8,128)(2,1)}) custom-call(s32[1,4,4]{2,1,0:T(4,128)} %pad_add_fusion.bounds, bf16[8,1024,128]{2,1,0:T(8,128)(2,1)} %fusion.49.q_ref, bf16[8,1024,128]{2,1,0:T(8,128)(2,1)} %fusion.50.k_ref, bf16[8,1024,128]{2,1,0:T(8,128)(2,1)} %fusion.29.v_ref, ...), custom_call_target="tpu_custom_call" | custom-call | flops 10737418240 | bytes 12582912 | tf_op jit(solution)/shard_map/attend_back/pallas_call | solution.py:193
  484.5 2.4 constant_dynamic-update-slice_fusion.5
  486.8 33.6 %attend_back.3 = (bf16[4,1024,128]{2,1,0:T(8,128)(2,1)}, bf16[4,1024,128]{2,1,0:T(8,128)(2,1)}, bf16[4,1024,128]{2,1,0:T(8,128)(2,1)}) custom-call(s32[1,4,4]{2,1,0:T(4,128)} %pad_add_fusion.bounds, bf16[8,1024,128]{2,1,0:T(8,128)(2,1)} %fusion.49.q_ref, bf16[8,1024,128]{2,1,0:T(8,128)(2,1)} %fusion.50.k_ref, bf16[8,1024,128]{2,1,0:T(8,128)(2,1)} %fusion.29.v_ref, ...), custom_call_target="tpu_custom_call" | custom-call | flops 10737418240 | bytes 12582912 | tf_op jit(solution)/shard_map/attend_back/pallas_call | solution.py:193
  520.4 2.3 constant_dynamic-update-slice_fusion.4
  522.7 4.1 convert_bitcast_fusion.1
  526.9 2.4 convert_bitcast_fusion
  529.7 2.4 copy.151
  533.4 1.4 constant_dynamic-update-slice_fusion
  534.8 2.4 convert_bitcast_fusion.3
  537.4 1.1 copy-done.15
  539.5 2.4 convert_bitcast_fusion.2
  542.1 2.1 fusion.52
  544.2 1.5 collective-permute-start
  547.2 23.8 %collective-permute-done.6 = f32[96,128]{1,0:T(8,128)S(1)} collective-permute-done((f32[96,128]{1,0:T(8,128)S(1)}, f32[96,128]{1,0:T(8,128)S(1)}, u32[]{:S(2)}, u32[]{:S(2)}) %collective-permute-start.6) | collective-permute-done | bytes 49184 | tf_op jit(solution)/shard_map/ppermute | solution.py:285
  571.0 48.9 %collective-permute-start.7 = (f32[96,128]{1,0:T(8,128)S(1)}, f32[96,128]{1,0:T(8,128)S(1)}, u32[]{:S(2)}, u32[]{:S(2)}) collective-permute-start(f32[96,128]{1,0:T(8,128)S(1)} %bitcast_add_fusion.8), channel_id=1, source_target_pairs={{0,8},{8,0},{1,9},{9,1},{2,10},{10,2},{3,11},{11,3},{4,12},{12,4},... | collective-permute-start | bytes 147464 | tf_op jit(solution)/shard_map/ppermute | solution.py:285
  619.9 3.1 collective-permute-done.7
  623.2 1.2 collective-permute-done.8
  624.5 1.9 collective-permute-start.3
  626.6 4.1 fusion.32
  630.7 3.3 collective-permute-done.3
  634.2 1.0 pad_maximum_fusion.1
  635.3 9.1 %collective-permute-done.1 = bf16[512,512]{1,0:T(8,128)(2,1)S(1)} collective-permute-done((bf16[512,512]{1,0:T(8,128)(2,1)}, bf16[512,512]{1,0:T(8,128)(2,1)S(1)}, u32[]{:S(2)}, u32[]{:S(2)}) %collective-permute-start.1) | collective-permute-done | bytes 524320 | tf_op jit(solution)/shard_map/ppermute | solution.py:275
  644.6 20.5 %bitcast_add_fusion.1 = f32[1024,2,512]{0,2,1:T(8,128)} fusion(f32[1024,2,512,1]{0,2,3,1:T(8,128)} %get-tuple-element.140, f32[1024,2,512]{0,2,1:T(8,128)} %bitcast.394, f32[1024,2,512,1]{0,2,3,1:T(8,128)} %get-tuple-element.139, bf16[1,8,1024,128]{3,2,1,0:T(8,128)(2,1)} %bitcast.414, bf16[1,8,1024,128]{3,2,1,0:T(8,128)(2,1)} %bitcast.418, ...), kind=kOutput, calls=%fused_computation.46 | convolution fusion | flops 6485442560 | bytes 35704832 | tf_op jit(solution)/shard_map/jntc,snjdc->std/dot_general | solution.py:291
  665.2 2.2 collective-permute-start.10
  667.3 5.8 add_convert_fusion
  673.1 4.0 copy.152
  677.1 5.4 copy.153
  683.2 1.5 collective-permute-start.5
  685.9 4.7 collective-permute-done.5
  691.7 31.8 %reduce-scatter.9.cloned.1.call-done = bf16[128,512]{1,0:T(8,128)(2,1)} async-done(((bf16[2048,512]{1,0:T(8,128)(2,1)}), bf16[128,512]{1,0:T(8,128)(2,1)}) %reduce-scatter.9.cloned.1.call-update) | async-done | bytes 131088 | tf_op jit(solution)/shard_map/reduce_scatter | solution.py:240
  723.5 1.5 collective-permute-start.4
  725.7 1.3 copy.155
  727.0 1.6 collective-permute-done.4
  729.8 1.1 copy.154
  (172 shorter events, 18.7 us)
Async XLA Ops:
  7.2 4.5 copy-start
  7.2 80.8 %all-gather.9.cloned.1.call-start = ((), (), s32[]{:S(2)}) async-start(), calls=%async_computation.8 | async-start | bytes 8912896 | tf_op jit(solution)/shard_map/all_gather | solution.py:217
  10.1 160.3 %all-gather.11.cloned.1.call-start = ((), (), s32[]{:S(2)}) async-start(), calls=%async_computation.9 | async-start | bytes 8912896 | tf_op jit(solution)/shard_map/all_gather | solution.py:217
  10.9 227.4 %all-gather.13.cloned.1.call-start = ((), (), s32[]{:S(2)}) async-start(), calls=%async_computation.10 | async-start | bytes 8912896 | tf_op jit(solution)/shard_map/all_gather | solution.py:217
  11.6 612.9 %reduce-scatter.7.cloned.1.call-start = ((), (), s32[]{:S(2)}) async-start(), calls=%async_computation.5 | async-start | bytes 4456448 | tf_op jit(solution)/shard_map/reduce_scatter | solution.py:240
  15.5 247.7 %copy-start.23 = (f32[2,512]{1,0:T(2,128)}, f32[2,512]{1,0:T(2,128)S(1)}, u32[]{:S(2)}) copy-start(f32[2,512]{1,0:T(2,128)S(1)} %mul.216) | copy-start | bytes 12292
  16.2 145.0 %copy-start.29 = (f32[2,512]{1,0:T(2,128)}, f32[2,512]{1,0:T(2,128)S(1)}, u32[]{:S(2)}) copy-start(f32[2,512]{1,0:T(2,128)S(1)} %add.298) | copy-start | bytes 12292
  16.9 221.4 %copy-start.31 = (f32[2,512]{1,0:T(2,128)}, f32[2,512]{1,0:T(2,128)S(1)}, u32[]{:S(2)}) copy-start(f32[2,512]{1,0:T(2,128)S(1)} %add.317) | copy-start | bytes 12292
  35.7 125.4 %copy-start.6 = (bf16[1024,1024]{0,1:T(8,128)(2,1)}, bf16[1024,1024]{0,1:T(8,128)(2,1)S(1)}, u32[]{:S(2)}) copy-start(bf16[1024,1024]{0,1:T(8,128)(2,1)S(1)} %copy.123) | copy-start | bytes 6291460
  167.9 2.0 copy-start.5
  255.4 3.5 copy-start.2
  255.4 7.7 %copy-start.21 = (f32[1024]{0:T(1024)}, f32[1024]{0:T(1024)S(1)}, u32[]{:S(2)}) copy-start(f32[1024]{0:T(1024)S(1)} %broadcast_multiply_fusion.4) | copy-start | bytes 12292
  258.3 4.9 copy-start.25
  258.9 4.3 copy-start.3
  263.1 1.1 copy-start.33
  263.2 1.1 copy-start.35
  264.2 18.6 %copy-start.12 = (f32[2,1024,512]{1,2,0:T(8,128)}, f32[2,1024,512]{1,2,0:T(8,128)S(1)}, u32[]{:S(2)}) copy-start(f32[2,1024,512]{1,2,0:T(8,128)S(1)} %subtract_multiply_fusion.1) | copy-start | bytes 12582916
  304.6 93.0 %collective-permute-start.2 = (bf16[16,256,512]{2,1,0:T(8,128)(2,1)}, bf16[16,256,512]{2,1,0:T(8,128)(2,1)}, u32[]{:S(2)}, u32[]{:S(2)}) collective-permute-start(bf16[16,256,512]{2,1,0:T(8,128)(2,1)} %dynamic-slice_bitcast_fusion), channel_id=1, source_target_pairs={{0,16},{16,0},{1,17},{17,1},{2,18},{18,2},{3,19},{19,3},{4,20},{20... | collective-permute-start | bytes 12582920 | tf_op jit(solution)/shard_map/ppermute | solution.py:253
  404.5 221.9 %reduce-scatter.5.cloned.1.call-start = ((), (), s32[]{:S(2)}) async-start(), calls=%async_computation.4 | async-start | bytes 8912896 | tf_op jit(solution)/shard_map/reduce_scatter | solution.py:240
  419.1 264.1 %reduce-scatter.11.cloned.1.call-start = ((), (), s32[]{:S(2)}) async-start(), calls=%async_computation.7 | async-start | bytes 4456448 | tf_op jit(solution)/shard_map/reduce_scatter | solution.py:240
  445.4 6.1 copy-start.13
  486.8 35.9 %copy-start.7 = (bf16[1024,1024]{0,1:T(8,128)(2,1)S(1)}, bf16[1024,1024]{0,1:T(8,128)(2,1)}, u32[]{:S(2)}) copy-start(bf16[1024,1024]{0,1:T(8,128)(2,1)} %copy-done.6) | copy-start | bytes 6291460
  522.7 4.2 copy-start.14
  522.7 4.2 copy-start.38
  532.1 1.2 copy-start.17
  532.2 191.3 %reduce-scatter.9.cloned.1.call-start = ((), (), s32[]{:S(2)}) async-start(), calls=%async_computation.6 | async-start | bytes 2228224 | tf_op jit(solution)/shard_map/reduce_scatter | solution.py:240
  534.8 11.0 %copy-start.11 = (bf16[8,1024,128]{2,1,0:T(8,128)(2,1)}, bf16[8,1024,128]{2,1,0:T(8,128)(2,1)S(1)}, u32[]{:S(2)}) copy-start(bf16[8,1024,128]{2,1,0:T(8,128)(2,1)S(1)} %constant_dynamic-update-slice_fusion) | copy-start | bytes 6291460
  537.2 1.2 copy-start.15
  537.2 1.5 copy-start.16
  537.2 2.2 copy-start.8
  539.5 2.4 copy-start.18
  542.1 4.0 copy-start.4
  542.1 4.0 copy-start.28
  542.1 4.0 copy-start.27
  542.1 4.1 copy-start.10
  542.1 81.1 %copy-start.37 = (f32[1024]{0:T(1024)S(1)}, f32[1024]{0:T(1024)}, u32[]{:S(2)}) copy-start(f32[1024]{0:T(1024)} %param.28) | copy-start | bytes 12292
  544.2 82.4 %collective-permute-start = (bf16[16,128,512]{2,1,0:T(8,128)(2,1)}, bf16[16,128,512]{2,1,0:T(8,128)(2,1)}, u32[]{:S(2)}, u32[]{:S(2)}) collective-permute-start(bf16[16,128,512]{2,1,0:T(8,128)(2,1)} %fusion.52), channel_id=1, source_target_pairs={{0,16},{16,0},{1,17},{17,1},{2,18},{18,2},{3,19},{19,3},{4,20},{20... | collective-permute-start | bytes 6291464 | tf_op jit(solution)/shard_map/ppermute | solution.py:253
  546.6 24.4 %collective-permute-start.6 = (f32[96,128]{1,0:T(8,128)S(1)}, f32[96,128]{1,0:T(8,128)S(1)}, u32[]{:S(2)}, u32[]{:S(2)}) collective-permute-start(f32[96,128]{1,0:T(8,128)S(1)} %bitcast.424), channel_id=1, source_target_pairs={{0,16},{16,0},{1,17},{17,1},{2,18},{18,2},{3,19},{19,3},{4,20},{20... | collective-permute-start | bytes 147464 | tf_op jit(solution)/shard_map/ppermute | solution.py:285
  571.0 52.1 %collective-permute-start.7 = (f32[96,128]{1,0:T(8,128)S(1)}, f32[96,128]{1,0:T(8,128)S(1)}, u32[]{:S(2)}, u32[]{:S(2)}) collective-permute-start(f32[96,128]{1,0:T(8,128)S(1)} %bitcast_add_fusion.8), channel_id=1, source_target_pairs={{0,8},{8,0},{1,9},{9,1},{2,10},{10,2},{3,11},{11,3},{4,12},{12,4},... | collective-permute-start | bytes 147464 | tf_op jit(solution)/shard_map/ppermute | solution.py:285
  623.1 1.3 collective-permute-start.8
  624.4 40.8 %collective-permute-start.9 = (f32[96,128]{1,0:T(8,128)S(1)}, f32[96,128]{1,0:T(8,128)S(1)}, u32[]{:S(2)}, u32[]{:S(2)}) collective-permute-start(f32[96,128]{1,0:T(8,128)S(1)} %add.344), channel_id=1, source_target_pairs={{0,2},{1,3},{2,0},{3,1},{4,6},{5,7},{6,4},{7,5},{8,10},{9,11},{10,... | collective-permute-start | bytes 147464 | tf_op jit(solution)/shard_map/ppermute | solution.py:285
  624.5 9.5 %copy-start.20 = (bf16[256,512]{1,0:T(8,128)(2,1)S(1)}, bf16[256,512]{1,0:T(8,128)(2,1)}, u32[]{:S(2)}) copy-start(bf16[256,512]{1,0:T(8,128)(2,1)} %reduce-scatter.7.cloned.1.call-done) | copy-start | bytes 786436
  624.5 9.5 %collective-permute-start.3 = (bf16[256,512]{1,0:T(8,128)(2,1)}, bf16[256,512]{1,0:T(8,128)(2,1)S(1)}, u32[]{:S(2)}, u32[]{:S(2)}) collective-permute-start(bf16[256,512]{1,0:T(8,128)(2,1)} %reduce-scatter.7.cloned.1.call-done), channel_id=1, source_target_pairs={{0,16},{16,0},{1,17},{17,1},{2,18},{18,2},{3,19},{19,3},{4,20},{20... | collective-permute-start | bytes 786440 | tf_op jit(solution)/shard_map/ppermute | solution.py:262
  626.4 18.0 %collective-permute-start.1 = (bf16[512,512]{1,0:T(8,128)(2,1)}, bf16[512,512]{1,0:T(8,128)(2,1)S(1)}, u32[]{:S(2)}, u32[]{:S(2)}) collective-permute-start(bf16[512,512]{1,0:T(8,128)(2,1)} %reduce-scatter.5.cloned.1.call-done), channel_id=1, source_target_pairs={{0,16},{16,0},{1,17},{17,1},{2,18},{18,2},{3,19},{19,3},{4,20},{20... | collective-permute-start | bytes 1572872 | tf_op jit(solution)/shard_map/ppermute | solution.py:275
  630.7 13.7 %copy-start.19 = (bf16[512,512]{1,0:T(8,128)(2,1)S(1)}, bf16[512,512]{1,0:T(8,128)(2,1)}, u32[]{:S(2)}) copy-start(bf16[512,512]{1,0:T(8,128)(2,1)} %reduce-scatter.5.cloned.1.call-done) | copy-start | bytes 1572868
  634.0 10.5 %copy-start.9 = (bf16[1024,1024]{0,1:T(8,128)(2,1)S(1)}, bf16[1024,1024]{0,1:T(8,128)(2,1)}, u32[]{:S(2)}) copy-start(bf16[1024,1024]{0,1:T(8,128)(2,1)} %copy-done.6) | copy-start | bytes 6291460
  634.1 10.5 %copy-start.22 = (f32[1024]{0:T(1024)S(1)}, f32[1024]{0:T(1024)}, u32[]{:S(2)}) copy-start(f32[1024]{0:T(1024)} %copy-done.21) | copy-start | bytes 12292
  634.1 10.5 %copy-start.24 = (f32[2,512]{1,0:T(2,128)S(1)}, f32[2,512]{1,0:T(2,128)}, u32[]{:S(2)}) copy-start(f32[2,512]{1,0:T(2,128)} %copy-done.23) | copy-start | bytes 12292
  634.1 10.5 %copy-start.26 = (f32[1024]{0:T(1024)S(1)}, f32[1024]{0:T(1024)}, u32[]{:S(2)}) copy-start(f32[1024]{0:T(1024)} %copy-done.25) | copy-start | bytes 12292
  634.1 10.5 %copy-start.30 = (f32[2,512]{1,0:T(2,128)S(1)}, f32[2,512]{1,0:T(2,128)}, u32[]{:S(2)}) copy-start(f32[2,512]{1,0:T(2,128)} %copy-done.29) | copy-start | bytes 12292
  634.1 10.5 %copy-start.32 = (f32[2,512]{1,0:T(2,128)S(1)}, f32[2,512]{1,0:T(2,128)}, u32[]{:S(2)}) copy-start(f32[2,512]{1,0:T(2,128)} %copy-done.31) | copy-start | bytes 12292
  634.1 10.5 %copy-start.34 = (f32[1024]{0:T(1024)S(1)}, f32[1024]{0:T(1024)}, u32[]{:S(2)}) copy-start(f32[1024]{0:T(1024)} %copy-done.33) | copy-start | bytes 12292
  634.1 10.5 %copy-start.36 = (f32[1024]{0:T(1024)S(1)}, f32[1024]{0:T(1024)}, u32[]{:S(2)}) copy-start(f32[1024]{0:T(1024)} %copy-done.35) | copy-start | bytes 12292
  665.2 17.3 %collective-permute-start.10 = (f32[96,128]{1,0:T(8,128)S(1)}, f32[96,128]{1,0:T(8,128)S(1)}, u32[]{:S(2)}, u32[]{:S(2)}) collective-permute-start(f32[96,128]{1,0:T(8,128)S(1)} %add.345), channel_id=1, source_target_pairs={{0,4},{1,5},{2,6},{3,7},{4,0},{5,1},{6,2},{7,3},{8,12},{9,13},{10,... | collective-permute-start | bytes 147464 | tf_op jit(solution)/shard_map/ppermute | solution.py:285
  683.2 7.4 %collective-permute-start.5 = (bf16[2,128,512]{2,1,0:T(8,128)(2,1)}, bf16[2,128,512]{2,1,0:T(8,128)(2,1)S(1)}, u32[]{:S(2)}, u32[]{:S(2)}) collective-permute-start(bf16[2,128,512]{2,1,0:T(8,128)(2,1)} %bitcast.420), channel_id=1, source_target_pairs={{0,16},{16,0},{1,17},{17,1},{2,18},{18,2},{3,19},{19,3},{4,20},{20... | collective-permute-start | bytes 786440 | tf_op jit(solution)/shard_map/ppermute | solution.py:275
  723.5 5.2 collective-permute-start.4
  725.0 5.9 copy-start.1
Sparse Core Ops, SparseCore 0:
  10.8 77.1 all-gather.8
  90.2 72.8 all-gather.10
  165.3 72.9 all-gather.12
  404.6 71.3 reduce-scatter.6
  479.9 102.5 reduce-scatter.4
  586.2 72.6 reduce-scatter.10
  662.6 60.8 reduce-scatter.8

commit v4 on v2

--- a/solution.py
+++ b/solution.py
@@ -202,6 +202,31 @@
         ),
         name="attend_back",
     )(bounds, q, k, v, q_mark, k_mark, lse, o, do)
+
+
+def grads_kernel(branch_ref, activ_ref, hidden_ref, pre_ref, o_ref):
+    o_ref[0] = jnp.dot(branch_ref[...], activ_ref[...], preferred_element_type=jnp.float32).astype(o_ref.dtype)
+    o_ref[1] = jnp.dot(hidden_ref[...], pre_ref[...], preferred_element_type=jnp.float32).astype(o_ref.dtype)
+
+
+def feed_forward_grads(branch, activ, hidden, pre):
+    shards, tokens, wide = branch.shape
+    tensors, _, deep = activ.shape
+    left = pl.BlockSpec((None, wide, tokens), lambda n, s: (s, 0, 0))
+    right = pl.BlockSpec((None, tokens, deep), lambda n, s: (n, 0, 0))
+    return pl.pallas_call(
+        grads_kernel,
+        grid=(tensors, shards),
+        in_specs=[left, right, left, right],
+        out_specs=pl.BlockSpec((None, None, 2, wide, deep), lambda n, s: (s, n, 0, 0, 0)),
+        out_shape=jax.ShapeDtypeStruct((shards, tensors, 2, wide, deep), jnp.bfloat16),
+        cost_estimate=pl.CostEstimate(
+            flops=4 * branch.size * tensors * deep,
+            bytes_accessed=4 * (branch.size + activ.size) + 4 * shards * tensors * wide * deep,
+            transcendentals=0,
+        ),
+        name="feed_forward_grads",
+    )(branch.swapaxes(1, 2), activ, hidden.swapaxes(1, 2), pre)
 
 
 def gather_blocks(weight):
@@ -364,14 +389,12 @@
     )
     down_bias_part = jnp.sum(resid_two_grad, axis=1)
     branch_grad = resid_two_grad.astype(jnp.bfloat16)
-    down_grad = dot("ntf,std->sndf", activ, branch_grad).astype(jnp.bfloat16)
-    down_owned = scatter_blocks(down_grad, down_weight.shape[::-1])
     activ_grad = dot("std,snfd->ntf", branch_grad, w_down)
     pre_grad = activ_grad * slope.astype(jnp.float32)
     up_bias_part = jnp.sum(pre_grad, axis=1)
     pre_low = pre_grad.astype(jnp.bfloat16)
-    up_grad = dot("ntf,std->sndf", pre_low, hidden_low).astype(jnp.bfloat16)
-    up_owned = scatter_blocks(up_grad, up_weight.shape)
+    ffn_grad = feed_forward_grads(branch_grad, activ, hidden_low, pre_low)
+    ffn_owned = scatter_blocks(ffn_grad, (2,) + up_weight.shape)
     back_middle = dot("ntf,sndf->std", pre_low, w_up)
     resid_one_grad, gain_one_grad, shift_one_grad = norm_back(
         resid_two_grad + back_middle, normed_one, spread_one, vec(norm1_gain)
@@ -393,8 +416,8 @@
     )
     back_input = dot("jntc,snjdc->std", proj_low, w_qkv)
     input_grad = resid_one_grad + back_input
-    down_owned = over_replicas(down_owned).T
-    up_owned = over_replicas(up_owned)
+    down_owned, up_owned = over_replicas(ffn_owned)
+    down_owned = down_owned.T
     attn_owned = over_replicas(attn_owned)
     qkv_owned, out_owned = attn_owned[:3].transpose(0, 2, 1), attn_owned[3]
     parts = (

time: 684 us -> 750 us (1.096)
  waiting for transfers between devices: 247 us -> 303 us
  Pallas kernels: 122 us -> 158 us
  matrix products: 163 us -> 132 us
    reduce_scatter x3 -> x2, waiting for transfers between devices: 137 us -> 186 us  [scatter_blocks(): owned = lax.psum_scatter(flat, OWNERS, scatter_dimension=0, tiled=True)]
    pallas_call x0 -> x1, Pallas kernels: none -> 36 us  [feed_forward_grads(): pl.pallas_call(grads_kernel, grid=(tensors, shards), in_specs=[left, righ...]
    dot_general x14 -> x12, matrix products: 163 us -> 132 us  [dot(): return jnp.einsum(spec, left, right, preferred_element_type=jnp.float32)]
    ppermute x3 -> x2, waiting for transfers between devices: 6.44 us -> 19.1 us  [over_replicas(): total = total + lax.ppermute(owned, 'replica', ring).astype(jnp.float32)]
    convert_element_type x0 -> x1, other arithmetic: none -> 7.53 us  [layer(): hidden_low = hidden_one.astype(jnp.bfloat16)]
    unnamed x109 -> x53, local copies, waits for them, and re-layouts: 19.6 us -> 18.9 us
  transfers between devices with their start and end apart: 14 -> 12, of which waited for: 8 -> 8; matrix products, arithmetic and copies ran while one was open for 28% -> 15% of each run, Pallas kernels for 18% -> 13%
where the time goes in v4:
time: 750 us; the launch traced here: 741 us
  waiting for transfers between devices  303 us (40%)
  Pallas kernels  158 us (21%)
  matrix products  132 us (18%)
  other arithmetic  40.8 us (5%)
  local copies, waits for them, and re-layouts  40.5 us (5%)
  starting transfers between devices  36 us (5%)
  blocking collectives  16 us (2%)
  between operations  14.7 us (2%)
    reduce_scatter x2, waiting for transfers between devices, scatter_blocks(): owned = lax.psum_scatter(flat, OWNERS, scatter_dimension=0, tiled=True)  186 us
    dot_general x12, matrix products, dot(): return jnp.einsum(spec, left, right, preferred_element_type=jnp.float32)  132 us
    all_gather x3, waiting for transfers between devices, gather_blocks(): blocks = lax.all_gather(weight, OWNERS, axis=0, tiled=False)  90.2 us
    pallas_call x1, Pallas kernels, attend_back(): pl.pallas_call(attend_back_kernel, grid_spec=pltpu.PrefetchScalarGridSpec...  63.1 us
    pallas_call x1, Pallas kernels, attend(): pl.pallas_call(attend_kernel, grid_spec=pltpu.PrefetchScalarGridSpec(num_...  58.9 us
    pallas_call x1, Pallas kernels, feed_forward_grads(): pl.pallas_call(grads_kernel, grid=(tensors, shards), in_specs=[left, righ...  36 us
    ppermute x5, starting transfers between devices, sum_over(): lax.ppermute(values, axis, [(i, i ^ step) for i in range(count)])  32.5 us
    ppermute x2, waiting for transfers between devices, over_replicas(): total = total + lax.ppermute(owned, 'replica', ring).astype(jnp.float32)  19.1 us
  transfers between devices with their start and end apart: 12, of which 8 were waited for; matrix products, arithmetic and copies ran while one was open for 15% of the time, Pallas kernels for 13%

profile of v4, /device:TPU:0, one launch (start us, length us, event | category | flops | bytes accessed | tf_op | source)
XLA Modules:
  0.0 740.7 jit_solution(6399550753817320991)
XLA Ops:
  7.2 1.0 copy.118
  8.3 1.8 pad_maximum_fusion.1
  10.2 0.7 all-gather.11.cloned.1.call-update
  11.9 0.8 slice_bitcast_fusion.19
  12.7 0.7 pad_maximum_fusion.2
  13.4 0.7 mul.222
  14.1 0.7 mul.243
  14.8 0.7 add.282
  15.4 0.7 add.275
  16.1 0.7 add.294
  16.8 16.0 %all-gather.4 = f32[8,1,768]{2,1,0:T(1,128)S(1)} all-gather(f32[1,1,768]{2,1,0:T(1,128)S(1)} %reshape.794), channel_id=3, replica_groups=mesh['replica'=2,'shard'=2,'tensor'=8] {'tensor'}, dimensions={0}, use_global_device_ids=true | all-gather | bytes 27648 | tf_op jit(solution)/shard_map/all_gather | solution.py:334
  32.9 2.9 copy.117
  35.7 4.8 copy.126
  41.4 1.0 fusion.97
  42.4 45.6 %all-gather.9.cloned.1.call-done = bf16[64,512,128]{2,1,0:T(8,128)(2,1)} async-done(((bf16[4,512,128]{2,1,0:T(8,128)(2,1)}), bf16[64,512,128]{2,1,0:T(8,128)(2,1)}) %all-gather.9.cloned.1.call-update) | async-done | bytes 8388624 | tf_op jit(solution)/shard_map/all_gather | solution.py:233
  88.0 9.2 %fusion.20 = f32[3,8,1024,128]{3,2,1,0:T(8,128)S(1)} fusion(bf16[2,1024,512,1,1]{1,2,0,3,4:T(8,128)(2,1)S(1)} %bitcast.392, bf16[2,8,4,512,128]{4,3,2,1,0:T(8,128)(2,1)} %bitcast.433), kind=kOutput, calls=%fused_computation.29 | convolution fusion | flops 6442450944 | bytes 20971520 | tf_op jit(solution)/shard_map/std,snjdc->jntc/dot_general | solution.py:282
  97.2 1.6 fusion.59.k_ref
  98.8 1.7 fusion.33.v_ref
  100.5 1.7 fusion.58.q_ref
  102.3 58.9 %attend.1 = (bf16[8,1024,128]{2,1,0:T(8,128)(2,1)}, f32[1,8,2,1024]{3,2,1,0:T(2,128)}) custom-call(s32[1,4,4]{2,1,0:T(4,128)} %pad_add_fusion.bounds, bf16[8,1024,128]{2,1,0:T(8,128)(2,1)} %fusion.58.q_ref, bf16[8,1024,128]{2,1,0:T(8,128)(2,1)} %fusion.59.k_ref, bf16[8,1024,128]{2,1,0:T(8,128)(2,1)} %fusion.33.v_ref, ...), custom_call_target="tpu_custom_call" | custom-call | flops 8589934592 | bytes 12582912 | tf_op jit(solution)/shard_map/attend/pallas_call | solution.py:161
  161.2 6.8 fusion.105
  167.9 1.9 copy-done.5
  170.4 23.2 %fusion.4 = (bf16[8,1024,512]{2,1,0:T(8,128)(2,1)}, bf16[8,1024,512]{2,1,0:T(8,128)(2,1)}) fusion(f32[8,512]{1,0:T(8,128)S(1)} %slice.138, bf16[2,8,512,512]{3,2,1,0:T(8,128)(2,1)} %bitcast.437, f32[2,1024,512]{1,2,0:T(8,128)} %copy-done.5, f32[2,512]{1,0:T(2,128)S(1)} %add.282, f32[2,512]{1,0:T(2,128)S(1)} %mul.222, f32[1024]{0:T(1024)S(1)} %add_rsqrt_fusion.1, ...), kind=kOutput, calls=%fused_computation.5 | convolution fusion | flops 8645509120 | bytes 29392896 | tf_op jit(solution)/shard_map/std,sndf->ntf/dot_general | solution.py:282
  193.6 44.6 %all-gather.13.cloned.1.call-done = bf16[8192,512]{1,0:T(8,128)(2,1)} async-done(((bf16[512,512]{1,0:T(8,128)(2,1)}), bf16[8192,512]{1,0:T(8,128)(2,1)}) %all-gather.13.cloned.1.call-update) | async-done | bytes 8388624 | tf_op jit(solution)/shard_map/all_gather | solution.py:233
  238.2 17.3 %fusion.103 = (f32[1024]{0:T(1024)S(1)}, f32[2,1024,512]{1,2,0:T(8,128)}, f32[1024,2,512,1]{0,2,3,1:T(8,128)}) fusion(f32[2,512]{1,0:T(2,128)S(1)} %add.294, f32[2,512]{1,0:T(2,128)S(1)} %add.282, f32[2,512]{1,0:T(2,128)S(1)} %mul.222, f32[1024]{0:T(1024)S(1)} %add_rsqrt_fusion.1, f32[2,1024,512]{1,2,0:T(8,128)} %copy-done.5, ...), kind=kOutput, calls=%fused_computation.186 | convolution fusion | flops 8597273600 | bytes 29384704 | tf_op jit(solution)/shard_map/ntf,snfd->std/dot_general | solution.py:282
  255.5 2.8 multiply_reduce_fusion.4
  258.9 3.5 multiply_reduce_fusion
  262.4 17.8 %fusion.6 = (f32[8,512]{1,0:T(8,128)S(1)}, bf16[8,1024,512]{2,1,0:T(8,128)(2,1)}) fusion(bf16[8,1024,512]{2,1,0:T(8,128)(2,1)} %get-tuple-element.23, bf16[2,8,512,512]{3,2,1,0:T(8,128)(2,1)} %bitcast.440, f32[2,1024,512]{1,2,0:T(8,128)} %get-tuple-element.98, f32[1024]{0:T(1024)S(1)} %broadcast_multiply_fusion.2, f32[1024]{0:T(1024)S(1)} %broadcast_multiply_fusion.3, ...), kind=kOutput, calls=%fused_computation.11 | convolution fusion | flops 8615096320 | bytes 33591296 | tf_op jit(solution)/shard_map/std,snfd->ntf/dot_general | solution.py:282
  280.3 19.0 %multiply_reduce_fusion.1 = (f32[2,512]{1,0:T(2,128)S(1)}, f32[1024]{0:T(1024)S(1)}, f32[1024]{0:T(1024)S(1)}, f32[2,512]{1,0:T(2,128)S(1)}, f32[2,1024,512]{1,2...) fusion(f32[2,1024,512]{1,2,0:T(8,128)} %copy-done.5, f32[1024]{0:T(1024)S(1)} %add_rsqrt_fusion.1, ...), kind=kOutput, calls=%fused_computation.71 | convolution fusion | flops 8608803840 | bytes 37801984 | tf_op jit(solution)/shard_map/ntf,sndf->std/dot_general | solution.py:282
  299.3 1.4 fusion.102
  300.8 5.5 fusion.90.do_ref
  306.3 3.8 convert_bitcast_fusion.1
  310.1 63.1 %attend_back.1 = (bf16[8,1024,128]{2,1,0:T(8,128)(2,1)}, bf16[8,1024,128]{2,1,0:T(8,128)(2,1)}, bf16[8,1024,128]{2,1,0:T(8,128)(2,1)}) custom-call(s32[1,4,4]{2,1,0:T(4,128)} %pad_add_fusion.bounds, bf16[8,1024,128]{2,1,0:T(8,128)(2,1)} %fusion.58.q_ref, bf16[8,1024,128]{2,1,0:T(8,128)(2,1)} %fusion.59.k_ref, bf16[8,1024,128]{2,1,0:T(8,128)(2,1)} %fusion.33.v_ref, ...), custom_call_target="tpu_custom_call" | custom-call | flops 21474836480 | bytes 25165824 | tf_op jit(solution)/shard_map/attend_back/pallas_call | solution.py:186
  373.2 4.1 convert_bitcast_fusion.4
  377.3 2.4 convert_bitcast_fusion.2
  379.8 2.4 convert_bitcast_fusion.3
  382.2 3.8 pad_maximum_fusion
  386.0 7.6 %copy.142 = bf16[2,8,4,128,512]{4,3,2,1,0:T(8,128)(2,1)} copy(bf16[2,8,4,128,512]{4,3,0,1,2:T(8,128)(2,1)} %pad_maximum_fusion) | data formatting | bytes 16777216 | tf_op jit(solution)/shard_map/stack | solution.py:413
  394.3 7.5 %fusion.89 = (bf16[2,512,1024]{2,1,0:T(8,128)(2,1)}, bf16[2,512,1024]{2,1,0:T(8,128)(2,1)}) fusion(f32[2,512]{1,0:T(2,128)S(1)} %add.282, f32[2,512]{1,0:T(2,128)S(1)} %mul.222, f32[1024]{0:T(1024)S(1)} %add_rsqrt_fusion.1, f32[1024]{0:T(1024)S(1)} %broadcast_multiply_fusion.5, f32[2,512]{1,0:T(2,128)S(1)} %copy-done.11, ...), kind=kLoop, calls=%fused_computation.117 | loop fusion | flops 18874368 | bytes 18919424 | tf_op jit(solution)/shard_map/convert_element_type | solution.py:378
  401.8 36.0 %feed_forward_grads.1 = bf16[2,8,2,512,512]{4,3,2,1,0:T(8,128)(2,1)} custom-call(bf16[2,512,1024]{2,1,0:T(8,128)(2,1)} %get-tuple-element.106.branch_ref, bf16[8,1024,512]{2,1,0:T(8,128)(2,1)} %get-tuple-element.22.activ_ref, bf16[2,512,1024]{2,1,0:T(8,128)(2,1)} %get-tuple-element.105.hidden_ref, bf16[8,1024,512]{2,1,0:T(8,128)(2,1)} %get-tuple-element.102.pre_ref), custom_call_target="tpu_custom_call" | custom-call | flops 17179869184 | bytes 37748736 | tf_op jit(solution)/shard_map/feed_forward_grads/pallas_call | solution.py:217
  437.9 2.1 convert_reduce_fusion.1
  440.0 1.9 convert_reduce_fusion
  442.1 1.6 collective-permute-start.1
  443.7 2.5 collective-permute-done.1
  446.2 28.0 %collective-permute-start.2 = (f32[96,128]{1,0:T(8,128)S(1)}, f32[96,128]{1,0:T(8,128)S(1)}, u32[]{:S(2)}, u32[]{:S(2)}) collective-permute-start(f32[96,128]{1,0:T(8,128)S(1)} %bitcast_add_fusion.8), channel_id=1, source_target_pairs={{0,8},{8,0},{1,9},{9,1},{2,10},{10,2},{3,11},{11,3},{4,12},{12,4},... | collective-permute-start | bytes 147464 | tf_op jit(solution)/shard_map/ppermute | solution.py:276
  474.2 2.2 collective-permute-done.2
  476.6 1.2 collective-permute-done.3
  477.8 2.2 collective-permute-start.4
  479.9 20.6 %bitcast_add_fusion.2 = f32[1024,2,512]{0,2,1:T(8,128)} fusion(f32[1024,2,512,1]{0,2,3,1:T(8,128)} %get-tuple-element.128, f32[1024,2,512]{0,2,1:T(8,128)} %bitcast.389, f32[1024,2,512,1]{0,2,3,1:T(8,128)} %get-tuple-element.127, bf16[1,8,1024,128]{3,2,1,0:T(8,128)(2,1)} %bitcast.404, bf16[1,8,1024,128]{3,2,1,0:T(8,128)(2,1)} %bitcast.441, ...), kind=kOutput, calls=%fused_computation.54 | convolution fusion | flops 6485442560 | bytes 35704832 | tf_op jit(solution)/shard_map/jntc,snjdc->std/dot_general | solution.py:282
  500.5 0.7 collective-permute-start.5
  501.2 5.9 add_convert_fusion
  507.1 3.9 copy.143
  511.0 5.4 copy.144
  516.4 7.5 %reduce-scatter.3.cloned.1.call-done = bf16[512,512]{1,0:T(8,128)(2,1)} async-done(((bf16[8192,512]{1,0:T(8,128)(2,1)}), bf16[512,512]{1,0:T(8,128)(2,1)}) %reduce-scatter.3.cloned.1.call-update) | async-done | bytes 524304 | tf_op jit(solution)/shard_map/reduce_scatter | solution.py:256
  523.9 1.7 collective-permute-start
  526.3 178.5 %reduce-scatter.5.cloned.1.call-done = bf16[1024,512]{1,0:T(8,128)(2,1)} async-done(((bf16[16384,512]{1,0:T(8,128)(2,1)}), bf16[1024,512]{1,0:T(8,128)(2,1)}) %reduce-scatter.5.cloned.1.call-update) | async-done | bytes 1048592 | tf_op jit(solution)/shard_map/reduce_scatter | solution.py:256
  704.8 1.5 collective-permute-start.6
  707.6 1.2 convert_add_fusion.2
  708.8 1.1 copy.145
  710.0 0.7 slice_bitcast_fusion.10
  710.7 19.1 %collective-permute-done.6 = bf16[2,512,512]{2,1,0:T(8,128)(2,1)} collective-permute-done((bf16[2,512,512]{2,1,0:T(8,128)(2,1)}, bf16[2,512,512]{2,1,0:T(8,128)(2,1)}, u32[]{:S(2)}, u32[]{:S(2)}) %collective-permute-start.6) | collective-permute-done | bytes 1048608 | tf_op jit(solution)/shard_map/ppermute | solution.py:266
  729.8 1.5 convert_add_fusion.1
  731.3 1.1 slice_bitcast_fusion.7
  732.4 1.3 copy.146
  (91 shorter events, 5.9 us)
Async XLA Ops:
  7.2 4.5 copy-start
  7.2 80.8 %all-gather.9.cloned.1.call-start = ((), (), s32[]{:S(2)}) async-start(), calls=%async_computation.4 | async-start | bytes 8912896 | tf_op jit(solution)/shard_map/all_gather | solution.py:233
  10.1 160.2 %all-gather.11.cloned.1.call-start = ((), (), s32[]{:S(2)}) async-start(), calls=%async_computation.5 | async-start | bytes 8912896 | tf_op jit(solution)/shard_map/all_gather | solution.py:233
  10.9 227.3 %all-gather.13.cloned.1.call-start = ((), (), s32[]{:S(2)}) async-start(), calls=%async_computation.6 | async-start | bytes 8912896 | tf_op jit(solution)/shard_map/all_gather | solution.py:233
  11.6 512.3 %reduce-scatter.3.cloned.1.call-start = ((), (), s32[]{:S(2)}) async-start(), calls=%async_computation.2 | async-start | bytes 8912896 | tf_op jit(solution)/shard_map/reduce_scatter | solution.py:256
  16.1 145.0 %copy-start.10 = (f32[2,512]{1,0:T(2,128)}, f32[2,512]{1,0:T(2,128)S(1)}, u32[]{:S(2)}) copy-start(f32[2,512]{1,0:T(2,128)S(1)} %add.275) | copy-start | bytes 12292
  35.7 125.4 %copy-start.3 = (bf16[1024,1024]{0,1:T(8,128)(2,1)}, bf16[1024,1024]{0,1:T(8,128)(2,1)S(1)}, u32[]{:S(2)}) copy-start(bf16[1024,1024]{0,1:T(8,128)(2,1)S(1)} %copy.117) | copy-start | bytes 6291460
  167.9 1.9 copy-start.5
  255.5 3.4 copy-start.2
  280.3 19.1 %copy-start.6 = (f32[2,1024,512]{1,2,0:T(8,128)S(1)}, f32[2,1024,512]{1,2,0:T(8,128)}, u32[]{:S(2)}) copy-start(f32[2,1024,512]{1,2,0:T(8,128)} %copy-done.5) | copy-start | bytes 12582916
  300.8 5.5 copy-start.14
  310.1 63.1 %copy-start.4 = (bf16[1024,1024]{0,1:T(8,128)(2,1)S(1)}, bf16[1024,1024]{0,1:T(8,128)(2,1)}, u32[]{:S(2)}) copy-start(bf16[1024,1024]{0,1:T(8,128)(2,1)} %copy-done.3) | copy-start | bytes 6291460
  373.2 4.1 copy-start.7
  377.3 2.4 copy-start.13
  379.7 2.4 copy-start.8
  393.6 0.7 copy-start.11
  393.6 311.2 %reduce-scatter.5.cloned.1.call-start = ((), (), s32[]{:S(2)}) async-start(), calls=%async_computation.3 | async-start | bytes 17825792 | tf_op jit(solution)/shard_map/reduce_scatter | solution.py:256
  437.8 38.7 %copy-start.12 = (f32[1024]{0:T(1024)S(1)}, f32[1024]{0:T(1024)}, u32[]{:S(2)}) copy-start(f32[1024]{0:T(1024)} %param.28) | copy-start | bytes 12292
  442.1 4.2 collective-permute-start.1
  446.2 30.2 %collective-permute-start.2 = (f32[96,128]{1,0:T(8,128)S(1)}, f32[96,128]{1,0:T(8,128)S(1)}, u32[]{:S(2)}, u32[]{:S(2)}) collective-permute-start(f32[96,128]{1,0:T(8,128)S(1)} %bitcast_add_fusion.8), channel_id=1, source_target_pairs={{0,8},{8,0},{1,9},{9,1},{2,10},{10,2},{3,11},{11,3},{4,12},{12,4},... | collective-permute-start | bytes 147464 | tf_op jit(solution)/shard_map/ppermute | solution.py:276
  476.5 1.3 collective-permute-start.3
  477.8 22.7 %collective-permute-start.4 = (f32[96,128]{1,0:T(8,128)S(1)}, f32[96,128]{1,0:T(8,128)S(1)}, u32[]{:S(2)}, u32[]{:S(2)}) collective-permute-start(f32[96,128]{1,0:T(8,128)S(1)} %add.310), channel_id=1, source_target_pairs={{0,2},{1,3},{2,0},{3,1},{4,6},{5,7},{6,4},{7,5},{8,10},{9,11},{10,... | collective-permute-start | bytes 147464 | tf_op jit(solution)/shard_map/ppermute | solution.py:276
  500.5 15.9 %collective-permute-start.5 = (f32[96,128]{1,0:T(8,128)S(1)}, f32[96,128]{1,0:T(8,128)S(1)}, u32[]{:S(2)}, u32[]{:S(2)}) collective-permute-start(f32[96,128]{1,0:T(8,128)S(1)} %add.311), channel_id=1, source_target_pairs={{0,4},{1,5},{2,6},{3,7},{4,0},{5,1},{6,2},{7,3},{8,12},{9,13},{10,... | collective-permute-start | bytes 147464 | tf_op jit(solution)/shard_map/ppermute | solution.py:276
  523.9 183.7 %collective-permute-start = (bf16[4,128,512]{2,1,0:T(8,128)(2,1)}, bf16[4,128,512]{2,1,0:T(8,128)(2,1)S(1)}, u32[]{:S(2)}, u32[]{:S(2)}) collective-permute-start(bf16[4,128,512]{2,1,0:T(8,128)(2,1)} %bitcast.407), channel_id=1, source_target_pairs={{0,16},{16,0},{1,17},{17,1},{2,18},{18,2},{3,19},{19,3},{4,20},{20... | collective-permute-start | bytes 1572872 | tf_op jit(solution)/shard_map/ppermute | solution.py:266
  704.8 24.9 %copy-start.9 = (bf16[1024,512]{1,0:T(8,128)(2,1)S(1)}, bf16[1024,512]{1,0:T(8,128)(2,1)}, u32[]{:S(2)}) copy-start(bf16[1024,512]{1,0:T(8,128)(2,1)} %reduce-scatter.5.cloned.1.call-done) | copy-start | bytes 3145732
  704.8 24.9 %collective-permute-start.6 = (bf16[2,512,512]{2,1,0:T(8,128)(2,1)}, bf16[2,512,512]{2,1,0:T(8,128)(2,1)}, u32[]{:S(2)}, u32[]{:S(2)}) collective-permute-start(bf16[2,512,512]{2,1,0:T(8,128)(2,1)} %bitcast.405), channel_id=1, source_target_pairs={{0,16},{16,0},{1,17},{17,1},{2,18},{18,2},{3,19},{19,3},{4,20},{20... | collective-permute-start | bytes 3145736 | tf_op jit(solution)/shard_map/ppermute | solution.py:266
  729.8 4.0 copy-start.1
Sparse Core Ops, SparseCore 0:
  10.8 77.1 all-gather.8
  90.2 72.8 all-gather.10
  165.3 72.8 all-gather.12
  393.7 130.1 reduce-scatter.2
  527.8 176.9 reduce-scatter.4
